TPU v7x, 32 devices: a whole 2x2x4 slice. The times are simulated.
32 devices in a mesh: ctx: 4 (over z), tp: 8 (over y, x, core).
Axes of the slice: x: 2, y: 2, z: 4, core: 2. Of those that a mesh axis runs over, the one named last changes fastest.
Arguments:
- hidden_in: bfloat16 [2, 1024, 4096], P(None, 'ctx', 'tp'), may hold values from -6 to 6
- decode_in: bfloat16 [2, 4096], replicated, may hold values from -6 to 6
- pre_len: int32 [2], replicated, may hold values from 1 to 2048, as said below
- new_len: int32 [2], replicated, may hold values from 1 to 1024, as said below
- key_cache: bfloat16 [2, 2048, 4096], P(None, 'ctx', 'tp'), may hold values from -120 to 120
- value_cache: bfloat16 [2, 2048, 4096], P(None, 'ctx', 'tp'), may hold values from -6 to 6
- ln_attn_gain: float32 [4096], replicated, may hold values from 0.1 to 1.9
- ln_attn_bias: float32 [4096], replicated, may hold values from -1.5 to 1.5
- ln_mlp_gain: float32 [4096], replicated, may hold values from 0.1 to 1.9
- ln_mlp_bias: float32 [4096], replicated, may hold values from -1.5 to 1.5
- qkv_weight: bfloat16 [3, 4096, 4096], P(None, None, 'tp'), may hold values from -0.09375 to 0.09375
- qkv_bias: float32 [3, 4096], P(None, 'tp'), may hold values from -1.5 to 1.5
- out_weight: bfloat16 [4096, 4096], P('tp'), may hold values from -0.09375 to 0.09375
- out_bias: float32 [4096], replicated, may hold values from -3 to 3
- up_weight: bfloat16 [4096, 12288], P(None, 'tp'), may hold values from -0.09375 to 0.09375
- up_bias: float32 [12288], P('tp'), may hold values from -3 to 3
- down_weight: bfloat16 [12288, 4096], P('tp'), may hold values from -0.0546875 to 0.0546875
- down_bias: float32 [4096], replicated, may hold values from -3 to 3
Outputs:
- prefill_out: bfloat16 [2, 1024, 4096], P(None, 'ctx', 'tp')
- new_keys: bfloat16 [2, 1024, 4096], P(None, 'ctx', 'tp')
- new_values: bfloat16 [2, 1024, 4096], P(None, 'ctx', 'tp')
- decode_out: bfloat16 [2, 4096], P(None, 'tp')
Inputs may be any that keep to these rules, and one draw needn't show every extreme that they name: `pre_len`: one sequence has a full cached prefix of 2048 slots; the others are shorter. `new_len`: one sequence has a full new prompt of 1024 slots; the others are shorter.
All inputs are finite; a program needn't handle non-finite values.
Results may differ from a plain program's by a relative error of at most 0.012.
Values may be sent and summed in bfloat16 or wider, within the bound.
No kernel may reach another device: no remote copies, remote signals or barrier semaphores. Data moves between devices by JAX's collectives and lax.ppermute only.
A program may use at most 192 MiB of HBM per device.

v0:
```python
import functools
import math

import jax
import jax.numpy as jnp
from jax import lax
from jax.experimental import pallas as pl
from jax.experimental.pallas import tpu as pltpu
from jax.sharding import PartitionSpec as P

HD = 128
ROT = 32


EPS = 1e-05
NEG = -1e30


def joined_2(part, axis, combine):
    gathered = jax.tree.map(lambda a: lax.all_gather(a, axis), part)

    def take(source):
        return jax.tree.map(lambda a: lax.dynamic_index_in_dim(a, source, 0, False), gathered)

    return lax.fori_loop(
        1, lax.axis_size(axis), lambda source, state: combine(state, take(source)), take(0)
    )


def norm_rows(rows, gain, shift):
    values = rows.astype(jnp.float32)
    center = values - jnp.mean(values, axis=-1, keepdims=True)
    spread = jnp.mean(center * center, axis=-1, keepdims=True)
    return (center * lax.rsqrt(spread + EPS) * gain + shift).astype(jnp.bfloat16)


def rotate(values, position):
    half = ROT // 2
    freqs = jnp.exp(jnp.arange(half, dtype=jnp.float32) * (-2.0 * math.log(10000.0) / ROT))
    angle = position.astype(jnp.float32)[..., None] * freqs
    cosine = jnp.cos(angle)
    sine = jnp.sin(angle)
    first = values[..., :half]
    second = values[..., half:ROT]
    return jnp.concatenate(
        [first * cosine - second * sine, second * cosine + first * sine, values[..., ROT:]], axis=-1
    )


def key_status(first, count, pre_dev, new_dev, pre_len, new_len):
    index = first + jnp.arange(count, dtype=jnp.int32)
    owner = index // (pre_dev + new_dev)
    offset = index % (pre_dev + new_dev)
    is_prefix = offset < pre_dev
    prefix_pos = owner * pre_dev + offset
    new_pos = owner * new_dev + offset - pre_dev
    prefix_ok = is_prefix[None, :] & (prefix_pos[None, :] < pre_len[:, None])
    new_ok = jnp.logical_not(is_prefix)[None, :] & (new_pos[None, :] < new_len[:, None])
    return (prefix_ok, new_ok, new_pos)


def absorb(state, queries, keys, values, allowed):
    top, total, acc = state
    scores = jnp.einsum("sqhd,skhd->shqk", queries, keys, preferred_element_type=jnp.float32) * (
        1.0 / math.sqrt(HD)
    )
    mask = allowed[:, None]
    scores = jnp.where(mask, scores, NEG)
    new_top = jnp.maximum(top, jnp.max(scores, axis=-1))
    weight = jnp.where(mask, jnp.exp(scores - new_top[..., None]), 0.0)
    factor = jnp.exp(top - new_top)
    total = total * factor + jnp.sum(weight, axis=-1)
    acc = acc * factor[..., None] + jnp.einsum(
        "shqk,skhd->shqd", weight.astype(jnp.bfloat16), values, preferred_element_type=jnp.float32
    )
    return (new_top, total, acc)


def empty_state(seqs, heads_dev, count):
    return (
        jnp.full((seqs, heads_dev, count), NEG, jnp.float32),
        jnp.zeros((seqs, heads_dev, count), jnp.float32),
        jnp.zeros((seqs, heads_dev, count, HD), jnp.float32),
    )


def join_parts(first, second):
    best = jnp.maximum(first[0], second[0])
    left = jnp.exp(first[0] - best)
    right = jnp.exp(second[0] - best)
    return (
        best,
        first[1] * left + second[1] * right,
        first[2] * left[..., None] + second[2] * right[..., None],
    )


def shards(
    hidden_in,
    decode_in,
    pre_len,
    new_len,
    key_cache,
    value_cache,
    ln_attn_gain,
    ln_attn_bias,
    ln_mlp_gain,
    ln_mlp_bias,
    qkv_weight,
    qkv_bias,
    out_weight,
    out_bias,
    up_weight,
    up_bias,
    down_weight,
    down_bias,
):
    seqs, new_dev, part_cols = hidden_in.shape
    pre_dev = key_cache.shape[1]
    local_cols = qkv_weight.shape[2]
    heads_dev = local_cols // HD
    width = decode_in.shape[1]
    block_len = pre_dev + new_dev
    rows_new = seqs * new_dev
    ctx_rank = lax.axis_index("ctx")
    tp_rank = lax.axis_index("tp")
    whole = lax.all_gather(hidden_in, "tp", axis=2, tiled=True)
    joined = jnp.concatenate([whole.reshape(rows_new, width), decode_in], axis=0)
    attn_in = norm_rows(joined, ln_attn_gain, ln_attn_bias)
    mlp_in = norm_rows(joined, ln_mlp_gain, ln_mlp_bias)
    proj = [
        jnp.dot(attn_in, qkv_weight[i], preferred_element_type=jnp.float32) + qkv_bias[i]
        for i in range(3)
    ]
    up_act = jax.nn.gelu(
        jnp.dot(mlp_in, up_weight, preferred_element_type=jnp.float32) + up_bias, approximate=False
    ).astype(jnp.bfloat16)
    query_index = ctx_rank * new_dev + jnp.arange(new_dev, dtype=jnp.int32)
    position = pre_len[:, None] + query_index[None, :]
    dec_position = pre_len + new_len
    q_new = rotate(
        proj[0][:rows_new].reshape(seqs, new_dev, heads_dev, HD), position[..., None]
    ).astype(jnp.bfloat16)
    k_new = rotate(
        proj[1][:rows_new].reshape(seqs, new_dev, heads_dev, HD), position[..., None]
    ).astype(jnp.bfloat16)
    v_new = proj[2][:rows_new].reshape(seqs, new_dev, heads_dev, HD).astype(jnp.bfloat16)
    q_dec = rotate(proj[0][rows_new:].reshape(seqs, heads_dev, HD), dec_position[:, None]).astype(
        jnp.bfloat16
    )
    k_dec = rotate(proj[1][rows_new:].reshape(seqs, heads_dev, HD), dec_position[:, None]).astype(
        jnp.bfloat16
    )
    v_dec = proj[2][rows_new:].reshape(seqs, heads_dev, HD).astype(jnp.bfloat16)
    live = query_index[None, :] < new_len[:, None]
    flat_keys = k_new.reshape(seqs, new_dev, local_cols)
    flat_values = v_new.reshape(seqs, new_dev, local_cols)
    new_keys = jnp.where(live[..., None], flat_keys, 0)
    new_values = jnp.where(live[..., None], flat_values, 0)
    local_block = jnp.concatenate(
        [jnp.stack([key_cache, value_cache], axis=2), jnp.stack([flat_keys, flat_values], axis=2)],
        axis=1,
    )
    local_keys = local_block[:, :, 0].reshape(seqs, block_len, heads_dev, HD)
    local_values = local_block[:, :, 1].reshape(seqs, block_len, heads_dev, HD)

    def allowed_for(first, count, queries_at):
        prefix_ok, new_ok, new_pos = key_status(first, count, pre_dev, new_dev, pre_len, new_len)
        return prefix_ok[:, None, :] | new_ok[:, None, :] & (
            new_pos[None, None, :] <= queries_at[None, :, None]
        )

    state = empty_state(seqs, heads_dev, new_dev)
    piece = lax.all_gather(local_block, "ctx", axis=1, tiled=True)
    blocks = piece.shape[1] // block_len

    def one_block(inner, number):
        begin = number * block_len
        slab = lax.dynamic_slice_in_dim(piece, begin, block_len, 1)
        keys = slab[:, :, 0].reshape(seqs, block_len, heads_dev, HD)
        values = slab[:, :, 1].reshape(seqs, block_len, heads_dev, HD)
        allowed = allowed_for(begin, block_len, query_index)
        return (absorb(inner, q_new, keys, values, allowed), None)

    state, _ = lax.scan(one_block, state, jnp.arange(blocks, dtype=jnp.int32))
    top, total, acc = state
    attn_new = (
        (acc / total[..., None])
        .transpose(0, 2, 1, 3)
        .reshape(rows_new, local_cols)
        .astype(jnp.bfloat16)
    )
    prefix_ok, new_ok, new_pos = key_status(
        ctx_rank * block_len, block_len, pre_dev, new_dev, pre_len, new_len
    )
    dec_allowed = (prefix_ok | new_ok)[:, None, :]
    dec_state = absorb(
        empty_state(seqs, heads_dev, 1), q_dec[:, None], local_keys, local_values, dec_allowed
    )
    dec_top, dec_total, dec_acc = joined_2(dec_state, "ctx", join_parts)
    dec_top = dec_top[..., 0]
    dec_total = dec_total[..., 0]
    dec_acc = dec_acc[:, :, 0]
    own = jnp.einsum("shd,shd->sh", q_dec, k_dec, preferred_element_type=jnp.float32) * (
        1.0 / math.sqrt(HD)
    )
    best = jnp.maximum(dec_top, own)
    far_factor = jnp.exp(dec_top - best)
    own_weight = jnp.exp(own - best)
    dec_total = dec_total * far_factor + own_weight
    dec_acc = dec_acc * far_factor[..., None] + jnp.einsum(
        "sh,shd->shd", own_weight.astype(jnp.bfloat16), v_dec, preferred_element_type=jnp.float32
    )
    attn_dec = (dec_acc / dec_total[..., None]).reshape(seqs, local_cols).astype(jnp.bfloat16)
    attn_rows = jnp.concatenate([attn_new, attn_dec], axis=0)
    branches = jnp.dot(attn_rows, out_weight, preferred_element_type=jnp.float32) + jnp.dot(
        up_act, down_weight, preferred_element_type=jnp.float32
    )
    summed_new, summed_dec = (
        lax.psum_scatter(
            branches[:rows_new].reshape(seqs, new_dev, width).astype(jnp.bfloat16),
            "tp",
            scatter_dimension=2,
            tiled=True,
        ).astype(jnp.float32),
        lax.psum_scatter(
            branches[rows_new:].astype(jnp.bfloat16), "tp", scatter_dimension=1, tiled=True
        ).astype(jnp.float32),
    )
    bias = lax.dynamic_slice_in_dim(out_bias + down_bias, tp_rank * part_cols, part_cols)
    prefill = hidden_in.astype(jnp.float32) + summed_new + bias
    prefill_out = jnp.where(live[..., None], prefill, 0.0).astype(jnp.bfloat16)
    dec_resid = lax.dynamic_slice_in_dim(decode_in, tp_rank * part_cols, part_cols, 1)
    decode_out = (dec_resid.astype(jnp.float32) + summed_dec + bias).astype(jnp.bfloat16)
    return (prefill_out, new_keys, new_values, decode_out)


BF = jnp.bfloat16
F32 = jnp.float32
DEC = 16
LSE = 16
SCALE = 1.0 / math.sqrt(HD)


def hop(value, axis, pairs):
    return lax.ppermute(value, axis, pairs)


def call(body, scal, ins, outs, scratch=(), limit=16, after=(), left=()):
    n, m = 1 + len(ins), len(after)
    left = [pltpu.with_memory_space_constraint(a, pltpu.HBM) for a in left]

    def run(*refs):
        body(*refs[: n + len(left)], *refs[n + len(left) + m :])

    return pl.pallas_call(
        run,
        out_shape=outs,
        in_specs=[pl.BlockSpec(memory_space=pltpu.SMEM)]
        + [pl.BlockSpec(memory_space=pltpu.VMEM)] * len(ins)
        + [pl.BlockSpec(memory_space=pltpu.HBM)] * len(left)
        + [pl.BlockSpec(memory_space=pl.ANY)] * m,
        out_specs=jax.tree.map(lambda _: pl.BlockSpec(memory_space=pltpu.VMEM), outs),
        scratch_shapes=list(scratch),
        compiler_params=pltpu.CompilerParams(vmem_limit_bytes=limit << 20),
    )(scal, *ins, *left, *after)


def struct(shape, dtype):
    return jax.ShapeDtypeStruct(tuple(shape), dtype)


ME, RANK, PRE, NEW = 0, 1, 2, 2 + DEC


def turn(values, table):
    cosine, down, up = (table[i] for i in range(3))
    parts = []
    for h in range(values.shape[1] // HD):
        one = values[:, h * HD : (h + 1) * HD]
        parts.append(
            one * cosine
            + pltpu.roll(one, HD - ROT // 2, 1) * down
            + pltpu.roll(one, ROT // 2, 1) * up
        )
    return jnp.concatenate(parts, axis=1)


def qkv_body(seqs, rows, part, sc, dec, norms, bias, table, *refs):
    weight, blocks = refs[0], refs[1:11]
    q_out, keys, values, values_t, k_dec, v_dec, mlp_in = refs[11:18]
    attn_in, held, hidden, sems, block_sems = refs[18:]
    moves = []
    for s in range(seqs):
        sources = [blocks[k].at[s] for k in range(6)] + [blocks[6 + s], blocks[8 + s]]
        moves.append(
            [
                pltpu.make_async_copy(source, hidden.at[s, k], block_sems.at[s, k])
                for k, source in enumerate(sources)
            ]
        )
        for move in moves[s]:
            move.start()
    copies = [pltpu.make_async_copy(weight.at[i], held.at[i], sems.at[i]) for i in range(3)]
    for copy in copies:
        copy.start()
    me = sc[ME]
    width = part * 8

    def finish(values, base, count, cols):
        total = functools.reduce(lambda a, b: a + b, values)
        mean = jnp.sum(total, axis=-1, keepdims=True) * (1.0 / width)
        values = [v - mean for v in values]
        square = functools.reduce(lambda a, b: a + b, [v * v for v in values])
        spread = jnp.sum(square, axis=-1, keepdims=True) * (1.0 / width)
        inv = lax.rsqrt(spread + EPS)
        for v, col in zip(values, cols, strict=True):
            v = v * inv
            at = pl.ds(col, part)
            attn_in[pl.ds(base, count), at] = (
                v * norms[pl.ds(0, 1), at] + norms[pl.ds(1, 1), at]
            ).astype(BF)
            mlp_in[pl.ds(base, count), at] = (
                v * norms[pl.ds(2, 1), at] + norms[pl.ds(3, 1), at]
            ).astype(BF)

    cols = [pl.multiple_of((me ^ k) * part, part) for k in range(8)]
    for s in range(seqs):
        for move in moves[s]:
            move.wait()

        def step(i, carry):
            at = pl.multiple_of(i * 16, 16)
            rows_of = [hidden[s, k, pl.ds(at, 16), :].astype(F32) for k in range(8)]
            finish(rows_of, pl.multiple_of(s * rows + at, 16), 16, cols)
            return carry

        lax.fori_loop(0, rows // 16, step, 0, unroll=4)
    tokens = [dec[:, pl.ds(k * part, part)].astype(F32) for k in range(8)]
    finish(tokens, seqs * rows, DEC, [k * part for k in range(8)])
    first = sc[RANK] * rows
    slot = lax.broadcasted_iota(jnp.int32, (rows, 1), 0) + first
    outs = []
    for i in range(3):
        copies[i].wait()
        out = jnp.dot(attn_in[...], held[i], preferred_element_type=F32) + bias[pl.ds(i, 1), :]
        if i < 2:
            out = turn(out, table)
        if i == 0:
            q_out[...] = out.astype(BF)
            continue
        for s in range(seqs):
            one = jnp.where(slot < sc[NEW + s], out[s * rows : (s + 1) * rows], 0.0)
            (keys if i == 1 else values)[s] = one.astype(BF)
            if i == 2:
                values_t[s] = jnp.transpose(one).astype(BF)
        (k_dec if i == 1 else v_dec)[...] = out[seqs * rows :].astype(BF)


def qkv(scal, blocks, dec, norms, weight, bias, table, after):
    seqs, rows, part = blocks[0].shape
    _, width, cols = weight.shape
    total = seqs * rows + DEC
    return call(
        functools.partial(qkv_body, seqs, rows, part),
        scal,
        [dec, norms, bias, table],
        (
            struct((total, cols), BF),
            *[struct((seqs, rows, cols), BF)] * 2,
            struct((seqs, cols, rows), BF),
            *[struct((DEC, cols), BF)] * 2,
            struct((total, width), BF),
        ),
        scratch=[
            pltpu.VMEM((total, width), BF),
            pltpu.VMEM((3, width, cols), BF),
            pltpu.VMEM((seqs, 8, rows, part), BF),
            pltpu.SemaphoreType.DMA((3,)),
            pltpu.SemaphoreType.DMA((seqs, 8)),
        ],
        limit=32,
        left=[weight, *blocks],
        after=after,
    )


def attend(query, pieces):
    scores = []
    for keys, _, limit in pieces:
        s = lax.dot_general(query, keys, (((1,), (1,)), ((), ())), preferred_element_type=F32)
        col = lax.broadcasted_iota(jnp.int32, s.shape, 1)
        scores.append(jnp.where(col < limit, s, NEG))
    top = functools.reduce(jnp.maximum, [jnp.max(s, axis=-1, keepdims=True) for s in scores])
    total = 0.0
    acc = 0.0
    for s, (_, values_t, _) in zip(scores, pieces, strict=True):
        weight = jnp.exp2((s - top) * (SCALE * math.log2(math.e)))
        total = total + jnp.sum(weight, axis=-1, keepdims=True)
        acc = acc + lax.dot_general(
            weight.astype(BF), values_t, (((1,), (1,)), ((), ())), preferred_element_type=F32
        )
    return acc / total, top * SCALE + jnp.log(total)


def attend_t(query, pieces):
    scores = []
    for keys, _, limit in pieces:
        s = lax.dot_general(keys, query, (((1,), (1,)), ((), ())), preferred_element_type=F32)
        row = lax.broadcasted_iota(jnp.int32, s.shape, 0)
        scores.append(jnp.where(row < limit, s, NEG))
    top = functools.reduce(jnp.maximum, [jnp.max(s, axis=0, keepdims=True) for s in scores])
    total = 0.0
    acc = 0.0
    for s, (_, values_t, _) in zip(scores, pieces, strict=True):
        weight = jnp.exp2((s - top) * (SCALE * math.log2(math.e)))
        total = total + jnp.sum(weight, axis=0, keepdims=True)
        acc = acc + jnp.dot(values_t, weight.astype(BF), preferred_element_type=F32)
    return acc / total, top * SCALE + jnp.log(total)


def pack_logs(logs):
    logs = jnp.concatenate(logs, axis=0)
    pieces = []
    for _ in range(3):
        short = logs.astype(BF).astype(F32)
        pieces.append(short)
        logs = logs - short
    return jnp.concatenate(pieces + [jnp.zeros_like(logs)], axis=0).astype(BF)


def unpack_logs(tile):
    tile = tile.astype(F32)
    return (tile[0:4] + tile[4:8]) + tile[8:12]


def head_slices(cols):
    return [slice(h * HD, (h + 1) * HD) for h in range(cols // HD)]


def attend_all(q, kc, vc, kn, vn, pre, new):
    found = []
    for at in head_slices(q.shape[1]):
        pieces = [(kc[:, at], vc[at, :], pre), (kn[:, at], vn[at, :], new)]
        found.append(attend_t(q[:, at], pieces))
    return found


def store_partial(out, heads, logs):
    cols = out.shape[0] - LSE
    for at, head in zip(head_slices(cols), heads, strict=True):
        out[at, :] = head.astype(BF)
    out[pl.ds(cols, LSE), :] = pack_logs(logs)


def limits(sc, seq, owner, asker, pre, rows):
    cached = sc[PRE + seq] - owner * pre
    col = lax.broadcasted_iota(jnp.int32, (1, rows), 1)
    fresh = jnp.minimum(sc[NEW + seq] - owner * rows, (asker - owner) * rows + col + 1)
    return cached, fresh


def own_body(seq, rows, pre, sc, q, kc, vc, kn, vn, out):
    rank = sc[RANK]
    found = attend_all(
        q.at[pl.ds(seq * rows, rows)],
        *(a.at[seq] for a in (kc, vc, kn, vn)),
        *limits(sc, seq, rank, rank, pre, rows),
    )
    store_partial(out, *zip(*found, strict=True))


def far_body(seq, rows, pre, sc, q, kc, vc, kn, vn, out):
    rank = sc[RANK]
    found = attend_all(
        q.at[seq],
        *(a.at[seq] for a in (kc, vc, kn, vn)),
        *limits(sc, seq, rank, rank ^ 3, pre, rows),
    )
    store_partial(out, *zip(*found, strict=True))


def attend_one(body, scal, seq, q, kv, after):
    pre, cols = kv[0].shape[1:]
    rows = kv[2].shape[1]
    return call(
        functools.partial(body, seq, rows, pre),
        scal,
        [q, *kv],
        struct((cols + LSE, rows), BF),
        after=after,
    )


def second_body(seq, rows, pre, sc, q, q_far, kc, vc, kn, vn, mine, mine_far, out, out_far):
    rank = sc[RANK]
    cols = kc.shape[2]
    for asker, source, before, target in (
        (rank ^ 3, q_far.at[seq], mine_far, out_far),
        (rank, q.at[pl.ds(seq * rows, rows)], mine, out),
    ):
        found = attend_all(
            source,
            kc.at[seq],
            vc.at[seq],
            kn.at[seq],
            vn.at[seq],
            *limits(sc, seq, rank ^ 1, asker, pre, rows),
        )
        earlier = unpack_logs(before[pl.ds(cols, LSE), :])
        heads, logs = [], []
        for h, at in enumerate(head_slices(cols)):
            head, log = found[h]
            old = earlier[h : h + 1]
            top = jnp.maximum(log, old)
            a, b = jnp.exp(log - top), jnp.exp(old - top)
            total = a + b
            heads.append((a / total) * head + (b / total) * before[at, :].astype(F32))
            logs.append(top + jnp.log(total))
        store_partial(target, heads, logs)


def attend_second(scal, seq, q, q_far, kv, mine, mine_far, after):
    pre, cols = kv[0].shape[1:]
    rows = kv[2].shape[1]
    return call(
        functools.partial(second_body, seq, rows, pre),
        scal,
        [q, q_far, *kv, mine, mine_far],
        (struct((cols + LSE, rows), BF),) * 2,
        after=after,
    )


def dec_body(seqs, rows, pre, sc, q, kc, vc, kn, vn, *refs):
    far, out = refs[:-1], refs[-1]
    far = [[a.at[s] for a in far] for s in range(seqs)]
    rank = sc[RANK]
    row = lax.broadcasted_iota(jnp.int32, (DEC, 1), 0)
    for at in head_slices(kc.shape[2]):
        result = jnp.zeros((DEC, HD), F32)
        log = jnp.full((DEC, HD), NEG, F32)
        for s in range(seqs):
            pieces = []
            mine = (kc.at[s], vc.at[s], kn.at[s], vn.at[s])
            for owner, (k, v, k2, v2) in ((rank, mine), (rank ^ 1, far[s])):
                pieces.append((k[:, at], v[at, :], sc[PRE + s] - owner * pre))
                pieces.append((k2[:, at], v2[at, :], sc[NEW + s] - owner * rows))
            one, one_log = attend(q[pl.ds(seqs * rows, DEC), at], pieces)
            result = jnp.where(row == s, one, result)
            log = jnp.where(row == s, jnp.broadcast_to(one_log, (DEC, HD)), log)
        out[pl.ds(0, DEC), at] = result
        out[pl.ds(DEC, DEC), at] = log


def attend_dec(scal, q, kv, far, after):
    seqs, pre, cols = kv[0].shape
    rows = kv[2].shape[1]
    return call(
        functools.partial(dec_body, seqs, rows, pre),
        scal,
        [q, *kv, *far],
        struct((2 * DEC, cols), F32),
        after=after,
    )


def blend(parts):
    cols = parts[0].shape[0] - LSE
    logs = [unpack_logs(ref[pl.ds(cols, LSE), :]) for ref in parts]
    top = functools.reduce(jnp.maximum, logs)
    weights = [jnp.exp(log - top) for log in logs]
    total = functools.reduce(lambda x, y: x + y, weights)
    heads = []
    for h, at in enumerate(head_slices(cols)):
        acc = 0.0
        for w, ref in zip(weights, parts, strict=True):
            acc = acc + (w / total)[h : h + 1] * ref[at, :].astype(F32)
        heads.append(acc)
    return heads


def decode_body(n, base, sc, q, k, v, *refs):
    parts, out = refs[:n], refs[n]
    for at in head_slices(k.shape[1]):
        both = q[pl.ds(base, DEC), at].astype(F32) * k[:, at].astype(F32)
        own = jnp.broadcast_to(jnp.sum(both, axis=-1, keepdims=True) * SCALE, (DEC, HD))
        logs = [p[pl.ds(DEC, DEC), at] for p in parts]
        top = functools.reduce(jnp.maximum, logs, own)
        share = jnp.exp(own - top)
        total = share
        acc = share.astype(BF).astype(F32) * v[:, at].astype(F32)
        for p, log in zip(parts, logs, strict=True):
            share = jnp.exp(log - top)
            total = total + share
            acc = acc + share * p[pl.ds(0, DEC), at]
        out[:, at] = (acc / total).astype(BF)


def decode_attn(scal, q, k_dec, v_dec, parts, after):
    return call(
        functools.partial(decode_body, len(parts), q.shape[0] - DEC),
        scal,
        [q, k_dec, v_dec, *parts],
        struct(k_dec.shape, BF),
        after=after,
    )


def fetch(weight, held, sems, tile):
    copies = []
    for i in range(weight.shape[1] // tile):
        at = (slice(None), pl.ds(i * tile, tile))
        copies.append(pltpu.make_async_copy(weight.at[at], held.at[at], sems.at[i]))
    for copy in copies:
        copy.start()
    return copies


def up_body(tile, sc, x, bias, weight, out, held, sems):
    fetch(weight, held, sems, tile)

    def step(i, carry):
        at = (slice(None), pl.ds(pl.multiple_of(i * tile, tile), tile))
        pltpu.make_async_copy(weight.at[at], held.at[at], sems.at[i]).wait()
        y = jnp.dot(x[...], held[at], preferred_element_type=F32) + bias[at]
        out[at] = (0.5 * y * (1.0 + lax.erf(y * math.sqrt(0.5)))).astype(BF)
        return carry

    lax.fori_loop(0, weight.shape[1] // tile, step, 0)


def up_proj(scal, x, weight, bias, after):
    total = x.shape[0]
    width, units = weight.shape
    tile = 512
    return call(
        functools.partial(up_body, tile),
        scal,
        [x, bias],
        struct((total, units), BF),
        scratch=[pltpu.VMEM(weight.shape, BF), pltpu.SemaphoreType.DMA((units // tile,))],
        limit=24,
        left=[weight],
        after=after,
    )


def down_body(tile, sc, x, weight, out, held, sems):
    for i, copy in enumerate(fetch(weight, held, sems, tile)):
        copy.wait()
        at = slice(i * tile, (i + 1) * tile)
        out[:, at] = jnp.dot(x[...], held[:, at], preferred_element_type=F32).astype(BF)


def down_proj(scal, x, weight, after):
    total = x.shape[0]
    units, width = weight.shape
    tile = 1024
    return call(
        functools.partial(down_body, tile),
        scal,
        [x],
        struct((total, width), BF),
        scratch=[pltpu.VMEM(weight.shape, BF), pltpu.SemaphoreType.DMA((width // tile,))],
        limit=24,
        left=[weight],
        after=after,
    )


def place(k):
    return (7 - k) // 2


def out_body(seq, tail, rows, part, sc, mine, far, *refs):
    if tail:
        dec, refs = refs[0], refs[1:]
    weight, mlp, odd, even, attn = refs
    for at, head in zip(head_slices(attn.shape[1]), blend([mine, far]), strict=True):
        attn[pl.ds(0, rows), at] = jnp.transpose(head).astype(BF)
    if tail:
        attn[pl.ds(rows, DEC), :] = dec[...]
    for j in range(8):
        k = sc[ME] ^ j
        at = slice(j * part, (j + 1) * part)
        out = jnp.dot(attn[...], weight[:, at], preferred_element_type=F32)
        base = mlp[pl.ds(seq * rows, rows), at].astype(F32)
        if tail:
            base = jnp.concatenate([base, mlp[pl.ds(mlp.shape[0] - DEC, DEC), at].astype(F32)], axis=0)
        out = (out + base).astype(BF)

        @pl.when(k % 2 == 1)
        def _():
            odd[place(k)] = out

        @pl.when(k % 2 == 0)
        def _():
            even[place(k)] = out


def out_proj(scal, seq, mine, far, dec, weight, mlp, after):
    cols, width = weight.shape
    rows = mine.shape[1]
    part = width // 8
    tail = dec is not None
    total = rows + (DEC if tail else 0)
    return call(
        functools.partial(out_body, seq, tail, rows, part),
        scal,
        [mine, far] + ([dec] if tail else []) + [weight, mlp],
        (struct((4, total, part), BF),) * 2,
        scratch=[pltpu.VMEM((total, cols), BF)],
        after=after,
    )


def swap(value, bit):
    return hop(value, "tp", [(i, i ^ bit) for i in range(8)])


def gather_rows(own, beside):
    x, y, c = swap(own, 2), swap(own, 4), swap(own, 1)
    x, y, beside = lax.optimization_barrier((x, y, beside))
    da, db = swap(y[0], 2), swap(x[1], 4)
    cx, cy = swap(x, 1), swap(y, 1)
    ca, cb = swap(da, 1), swap(db, 1)
    return [own, c, x, cx, y, cy, da, db, ca, cb], beside


def scatter_rows(odd, even, rows):
    half = rows // 2

    def both(a, b):
        return a.astype(F32) + b.astype(F32)

    other = swap(odd, 1)
    far = both(even[0], other[0]).astype(BF)
    got_y, got_x = swap(far[:half], 2), swap(far[half:], 4)
    to_y = both(even[1], other[1])
    to_y = jnp.concatenate([to_y[:half] + got_y.astype(F32), to_y[half:]], axis=0).astype(BF)
    to_x = both(even[2], other[2])
    to_x = jnp.concatenate([to_x[:half], to_x[half:] + got_x.astype(F32)], axis=0).astype(BF)
    from_x, from_y = swap(to_x, 2), swap(to_y, 4)
    return both(even[3], other[3]) + both(from_x, from_y)


def rope_table(position):
    lane = jnp.arange(HD, dtype=jnp.int32)
    half = ROT // 2
    freqs = jnp.exp((lane % half).astype(F32) * (-2.0 * math.log(10000.0) / ROT))
    angle = position.astype(F32)[:, None] * freqs[None, :]
    cosine = jnp.where(lane < ROT, jnp.cos(angle), 1.0)
    sine = jnp.sin(angle)
    down = jnp.where(lane < half, -sine, 0.0)
    up = jnp.where((lane >= half) & (lane < ROT), sine, 0.0)
    return jnp.stack([cosine, down, up])


def moved_queries(
    hidden_in,
    decode_in,
    pre_len,
    new_len,
    key_cache,
    value_cache,
    ln_attn_gain,
    ln_attn_bias,
    ln_mlp_gain,
    ln_mlp_bias,
    qkv_weight,
    qkv_bias,
    out_weight,
    out_bias,
    up_weight,
    up_bias,
    down_weight,
    down_bias,
):
    seqs, rows, part = hidden_in.shape
    n = lax.axis_size("ctx")
    rank = lax.axis_index("ctx")
    me = lax.axis_index("tp")
    mate = [(i, i ^ 1) for i in range(n)]
    across = [(i, i ^ 3) for i in range(n)]
    room = (0, DEC - seqs)
    scal = jnp.concatenate([jnp.stack([me, rank]), jnp.pad(pre_len, room), jnp.pad(new_len, room)])
    norms = jnp.stack([ln_attn_gain, ln_attn_bias, ln_mlp_gain, ln_mlp_bias])
    dec_rows = jnp.pad(decode_in, (room, (0, 0)))
    index = rank * rows + jnp.arange(rows, dtype=jnp.int32)
    position = [pre_len[s] + index for s in range(seqs)] + [jnp.pad(pre_len + new_len, room)]
    table = rope_table(jnp.concatenate(position))

    values_t = jnp.swapaxes(value_cache, 1, 2)
    far_k = hop(key_cache, "ctx", mate)
    far_v = hop(values_t, "ctx", mate)
    blocks, (table, dec_rows, norms) = gather_rows(hidden_in, (table, dec_rows, norms))
    q, new_keys, new_values, new_values_t, k_dec, v_dec, mlp_in = qkv(
        scal, blocks, dec_rows, norms, qkv_weight, qkv_bias, table, [far_k]
    )
    q_far = hop(q[: seqs * rows].reshape(seqs, rows, -1), "ctx", across)
    kv = (key_cache, values_t, new_keys, new_values_t)
    far_kv = (far_k, far_v, hop(new_keys, "ctx", mate), hop(new_values_t, "ctx", mate))

    up = up_proj(scal, mlp_in, up_weight, up_bias[None, :], [])
    own, far, last = [], [], [up, far_v]
    for s in range(seqs):
        own.append(attend_one(own_body, scal, s, q, kv, last))
        last = [own[s]]
    for s in range(seqs):
        far.append(attend_one(far_body, scal, s, q_far, kv, last))
        last = [far[s]]
    mlp = down_proj(scal, up, down_weight, last)
    last = [mlp]
    ends = []
    for s in range(seqs):
        mine, back = attend_second(scal, s, q, q_far, far_kv, own[s], far[s], last)
        last = [back]
        ends.append((mine, hop(back, "ctx", across)))
    dec = attend_dec(scal, q, kv, far_kv, last)
    dec_far = hop(dec, "ctx", across)
    attn_dec = decode_attn(scal, q, k_dec, v_dec, [dec, dec_far], [ends[-1][1]])
    last = attn_dec

    bias = lax.dynamic_slice_in_dim(out_bias + down_bias, me * part, part)
    prefill = []
    for s in range(seqs):
        odd, even = out_proj(
            scal, s, *ends[s], attn_dec if s == seqs - 1 else None, out_weight, mlp, [last]
        )
        last = even
        summed = scatter_rows(odd, even, rows)
        live = index < new_len[s]
        full = hidden_in[s].astype(F32) + summed[:rows] + bias
        prefill.append(jnp.where(live[:, None], full, 0.0).astype(BF))
        if s == seqs - 1:
            resid = lax.dynamic_slice_in_dim(decode_in, me * part, part, 1)
            decode_out = (resid.astype(F32) + summed[rows : rows + seqs] + bias).astype(BF)
    return (jnp.stack(prefill), new_keys, new_values, decode_out)


def layer(ctx, tp, *args):
    seqs, rows, part = args[0].shape
    pre, cols = args[4].shape[1:]
    if tp == 8 and ctx == 4 and seqs == 2 and rows % HD == 0 and pre % HD == 0 and cols == 4 * HD:
        return moved_queries(*args)
    return shards(*args)


def solution(mesh):
    return jax.shard_map(
        functools.partial(layer, mesh.shape["ctx"], mesh.shape["tp"]),
        mesh=mesh,
        in_specs=(
            P(None, "ctx", "tp"),
            P(),
            P(),
            P(),
            P(None, "ctx", "tp"),
            P(None, "ctx", "tp"),
            P(),
            P(),
            P(),
            P(),
            P(None, None, "tp"),
            P(None, "tp"),
            P("tp", None),
            P(),
            P(None, "tp"),
            P("tp"),
            P("tp", None),
            P(),
        ),
        out_specs=(P(None, "ctx", "tp"), P(None, "ctx", "tp"), P(None, "ctx", "tp"), P(None, "tp")),
        check_vma=False,
    )
```

profile of v0, /device:TPU:16, one launch (start us, length us, event | category | flops | bytes accessed | tf_op | source)
XLA Modules:
  0.0 162.1 jit_solution(5635004468314567170)
XLA Ops:
  0.7 1.6 collective-permute-start
  2.2 1.5 collective-permute-start.1
  3.8 1.6 collective-permute-start.9
  11.6 3.1 %collective-permute-done.refs_8_ = bf16[2,256,512]{2,1,0:T(8,128)(2,1)} collective-permute-done((bf16[2,256,512]{2,1,0:T(8,128)(2,1)}, bf16[2,256,512]{2,1,0:T(8,128)(2,1)}, u32[]{:S(2)}, u32[]{:S(2)}) %collective-permute-start) | collective-permute-done | bytes 524320 | tf_op jit(solution)/shard_map/ppermute | solution.py:246
  17.5 1.7 %slice_bitcast_fusion.4 = bf16[256,512]{1,0:T(8,128)(2,1)} fusion(bf16[2,256,512]{2,1,0:T(8,128)(2,1)} %collective-permute-done.refs_8_), kind=kLoop, calls=%fused_computation.46 | loop fusion | bytes 524288 | tf_op jit(solution)/shard_map/squeeze | solution.py:725
  19.2 1.5 collective-permute-start.6
  20.7 3.2 %collective-permute-done.5.refs_12_ = bf16[256,512]{1,0:T(8,128)(2,1)} collective-permute-done((bf16[256,512]{1,0:T(8,128)(2,1)S(1)}, bf16[256,512]{1,0:T(8,128)(2,1)}, u32[]{:S(2)}, u32[]{:S(2)}) %collective-permute-start.5) | collective-permute-done | bytes 262176 | tf_op jit(solution)/shard_map/ppermute | solution.py:246
  26.1 1.6 collective-permute-start.11
  27.8 1.8 %collective-permute-done.8.refs_15_ = bf16[256,512]{1,0:T(8,128)(2,1)} collective-permute-done((bf16[256,512]{1,0:T(8,128)(2,1)}, bf16[256,512]{1,0:T(8,128)(2,1)}, u32[]{:S(2)}, u32[]{:S(2)}) %collective-permute-start.8) | collective-permute-done | bytes 262176 | tf_op jit(solution)/shard_map/ppermute | solution.py:246
  31.1 15.3 %shard_map.201 = (bf16[528,512]{1,0:T(8,128)(2,1)S(1)}, bf16[2,256,512]{2,1,0:T(8,128)(2,1)}, bf16[2,256,512]{2,1,0:T(8,128)(2,1)}, bf16[2,512,256]{2,1,0:T(8,12...) custom-call(s32[34]{0:T(128)S(1)} %pad_add_fusion.1.refs_0_, ...), custom_call_target="tpu_custom_call" | custom-call | tf_op jit(solution)/shard_map/pallas_call | solution.py:256
  48.9 10.5 %shard_map.202.refs_6_.refs_1_ = bf16[528,1536]{1,0:T(8,128)(2,1)S(1)} custom-call(s32[34]{0:T(128)S(1)} %pad_add_fusion.1.refs_0_, bf16[528,4096]{1,0:T(8,128)(2,1)S(1)} %get-tuple-element.32.refs_1_, f32[1,1536]{1,0:T(1,128)S(1)} %broadcast_in_dim.52.refs_2_, bf16[4096,1536]{1,0:T(8,128)(2,1)} %refs_3_.4), custom_call_target="tpu_custom_call" | custom-call | tf_op jit(solution)/shard_map/pallas_call | solution.py:256
  59.4 3.0 %collective-permute-done.11.refs_7_.refs_4_ = bf16[2,512,512]{2,1,0:T(8,128)(2,1)S(1)} collective-permute-done((bf16[2,512,512]{2,1,0:T(8,128)(2,1)S(1)}, bf16[2,512,512]{2,1,0:T(8,128)(2,1)S(1)}, u32[]{:S(2)}, u32[]{:S(2)}) %collective-permute-start.11) | collective-permute-done | bytes 1048608 | tf_op jit(solution)/shard_map/ppermute | solution.py:246
  62.4 2.6 %shard_map.203.refs_6_.refs_7_ = bf16[528,256]{1,0:T(8,128)(2,1)S(1)} custom-call(s32[34]{0:T(128)S(1)} %pad_add_fusion.1.refs_0_, bf16[528,512]{1,0:T(8,128)(2,1)S(1)} %get-tuple-element.29.refs_1_, bf16[2,512,512]{2,1,0:T(8,128)(2,1)S(1)} %copy-done, bf16[2,512,512]{2,1,0:T(8,128)(2,1)S(1)} %bitcast.75, bf16[2,256,512]{2,1,0:T(8,128)(2,1)S(1)} %copy-done.2, ...), custom_call_target="tpu_custom_call" | custom-call | tf_op jit(solution)/shard_map/pallas_call | solution.py:256
  65.0 2.6 %shard_map.204.refs_6_.refs_7_ = bf16[528,256]{1,0:T(8,128)(2,1)S(1)} custom-call(s32[34]{0:T(128)S(1)} %pad_add_fusion.1.refs_0_, bf16[528,512]{1,0:T(8,128)(2,1)S(1)} %get-tuple-element.29.refs_1_, bf16[2,512,512]{2,1,0:T(8,128)(2,1)S(1)} %copy-done, bf16[2,512,512]{2,1,0:T(8,128)(2,1)S(1)} %bitcast.76, bf16[2,256,512]{2,1,0:T(8,128)(2,1)S(1)} %copy-done.2, ...), custom_call_target="tpu_custom_call" | custom-call | tf_op jit(solution)/shard_map/pallas_call | solution.py:256
  67.7 3.6 %collective-permute-done.10.refs_1_.refs_2_ = bf16[2,256,512]{2,1,0:T(8,128)(2,1)S(1)} collective-permute-done((bf16[2,256,512]{2,1,0:T(8,128)(2,1)S(1)}, bf16[2,256,512]{2,1,0:T(8,128)(2,1)S(1)}, u32[]{:S(2)}, u32[]{:S(2)}) %collective-permute-start.10) | collective-permute-done | bytes 524320 | tf_op jit(solution)/shard_map/ppermute | solution.py:246
  71.3 2.6 %shard_map.205.refs_6_.refs_8_ = bf16[528,256]{1,0:T(8,128)(2,1)S(1)} custom-call(s32[34]{0:T(128)S(1)} %pad_add_fusion.1.refs_0_, bf16[2,256,512]{2,1,0:T(8,128)(2,1)S(1)} %collective-permute-done.10.refs_1_.refs_2_, bf16[2,512,512]{2,1,0:T(8,128)(2,1)S(1)} %copy-done, bf16[2,512,512]{2,1,0:T(8,128)(2,1)S(1)} %bitcast.77, ...), custom_call_target="tpu_custom_call" | custom-call | tf_op jit(solution)/shard_map/pallas_call | solution.py:256
  74.0 2.6 %shard_map.206.refs_3_.refs_8_ = bf16[528,256]{1,0:T(8,128)(2,1)S(1)} custom-call(s32[34]{0:T(128)S(1)} %pad_add_fusion.1.refs_0_, bf16[2,256,512]{2,1,0:T(8,128)(2,1)S(1)} %collective-permute-done.10.refs_1_.refs_2_, bf16[2,512,512]{2,1,0:T(8,128)(2,1)S(1)} %copy-done, bf16[2,512,512]{2,1,0:T(8,128)(2,1)S(1)} %bitcast.78, ...), custom_call_target="tpu_custom_call" | custom-call | tf_op jit(solution)/shard_map/pallas_call | solution.py:256
  76.6 10.0 %shard_map.207.refs_9_.refs_4_.refs_5_ = bf16[528,4096]{1,0:T(8,128)(2,1)S(1)} custom-call(s32[34]{0:T(128)S(1)} %pad_add_fusion.1.refs_0_, bf16[528,1536]{1,0:T(8,128)(2,1)S(1)} %shard_map.202.refs_6_.refs_1_, bf16[1536,4096]{1,0:T(8,128)(2,1)} %refs_2_.10, bf16[528,256]{1,0:T(8,128)(2,1)S(1)} %shard_map.206.refs_3_.refs_8_), custom_call_target="tpu_custom_call" | custom-call | tf_op jit(solution)/shard_map/pallas_call | solution.py:256
  86.6 4.7 %shard_map.208 = (bf16[528,256]{1,0:T(8,128)(2,1)S(1)}, bf16[528,256]{1,0:T(8,128)(2,1)S(1)}) custom-call(s32[34]{0:T(128)S(1)} %pad_add_fusion.1.refs_0_, bf16[528,512]{1,0:T(8,128)(2,1)S(1)} %get-tuple-element.29.refs_1_, bf16[2,256,512]{2,1,0:T(8,128)(2,1)S(1)} %collective-permute-done.10.refs_1_.refs_2_, ...), custom_call_target="tpu_custom_call" | custom-call | tf_op jit(solution)/shard_map/pallas_call | solution.py:256
  91.2 4.4 %shard_map.209 = (bf16[528,256]{1,0:T(8,128)(2,1)S(1)}, bf16[528,256]{1,0:T(8,128)(2,1)S(1)}) custom-call(s32[34]{0:T(128)S(1)} %pad_add_fusion.1.refs_0_, bf16[528,512]{1,0:T(8,128)(2,1)S(1)} %get-tuple-element.29.refs_1_, bf16[2,256,512]{2,1,0:T(8,128)(2,1)S(1)} %collective-permute-done.10.refs_1_.refs_2_, ...), custom_call_target="tpu_custom_call" | custom-call | tf_op jit(solution)/shard_map/pallas_call | solution.py:256
  96.0 1.7 %collective-permute-start.14 = (bf16[528,256]{1,0:T(8,128)(2,1)S(1)}, bf16[528,256]{1,0:T(8,128)(2,1)S(1)}, u32[]{:S(2)}, u32[]{:S(2)}) collective-permute-start(bf16[528,256]{1,0:T(8,128)(2,1)S(1)} %get-tuple-element.34.refs_9_), channel_id=1, source_target_pairs={{0,24},{8,16},{16,8},{24,0},{1,25},{9,17},{17,9},{25,1},{2,26},{10... | collective-permute-start | bytes 811016 | tf_op jit(solution)/shard_map/ppermute | solution.py:246
  97.8 2.6 %shard_map.210.refs_4_ = f32[32,512]{1,0:T(8,128)S(1)} custom-call(s32[34]{0:T(128)S(1)} %pad_add_fusion.1.refs_0_, bf16[528,512]{1,0:T(8,128)(2,1)S(1)} %get-tuple-element.29.refs_1_, bf16[2,512,512]{2,1,0:T(8,128)(2,1)S(1)} %copy-done, bf16[2,512,512]{2,1,0:T(8,128)(2,1)S(1)} %bitcast.79, bf16[2,256,512]{2,1,0:T(8,128)(2,1)S(1)} %copy-done.2, ...), custom_call_target="tpu_custom_call" | custom-call | tf_op jit(solution)/shard_map/pallas_call | solution.py:256
  100.7 22.6 %collective-permute-done.15.refs_5_ = f32[32,512]{1,0:T(8,128)S(1)} collective-permute-done((f32[32,512]{1,0:T(8,128)S(1)}, f32[32,512]{1,0:T(8,128)S(1)}, u32[]{:S(2)}, u32[]{:S(2)}) %collective-permute-start.15) | collective-permute-done | bytes 65568 | tf_op jit(solution)/shard_map/ppermute | solution.py:246
  124.0 4.3 %shard_map.212 = (bf16[4,256,512]{2,1,0:T(8,128)(2,1)}, bf16[4,256,512]{2,1,0:T(8,128)(2,1)S(1)}) custom-call(s32[34]{0:T(128)S(1)} %pad_add_fusion.1.refs_0_, bf16[528,256]{1,0:T(8,128)(2,1)S(1)} %get-tuple-element.33.refs_1_, bf16[528,256]{1,0:T(8,128)(2,1)S(1)} %collective-permute-done.14.refs_2_, bf16[512,4096]{1,0:T(8,128)(2,1)S(1)} %copy-done.1, ...), custom_call_target="tpu_custom_call" | custom-call | tf_op jit(solution)/shard_map/pallas_call | solution.py:256
  128.8 3.4 %shard_map.213 = (bf16[4,272,512]{2,1,0:T(8,128)(2,1)S(1)}, bf16[4,272,512]{2,1,0:T(8,128)(2,1)S(1)}) custom-call(s32[34]{0:T(128)S(1)} %pad_add_fusion.1.refs_0_, bf16[528,256]{1,0:T(8,128)(2,1)S(1)} %get-tuple-element.40.refs_1_, bf16[528,256]{1,0:T(8,128)(2,1)S(1)} %collective-permute-done.16.refs_6_.refs_2_, ...), custom_call_target="tpu_custom_call" | custom-call | tf_op jit(solution)/shard_map/pallas_call | solution.py:256
  136.2 1.9 %collective-permute-start.18 = (bf16[128,512]{1,0:T(8,128)(2,1)S(1)}, bf16[128,512]{1,0:T(8,128)(2,1)S(1)}, u32[]{:S(2)}, u32[]{:S(2)}) collective-permute-start(bf16[128,512]{1,0:T(8,128)(2,1)S(1)} %get-tuple-element.52), channel_id=1, source_target_pairs={{0,4},{1,5},{2,6},{3,7},{4,0},{5,1},{6,2},{7,3},{8,12},{9,13},{10,... | collective-permute-start | bytes 393224 | tf_op jit(solution)/shard_map/ppermute | solution.py:246
  139.9 1.5 collective-permute-start.23
  142.0 1.7 %collective-permute-start.19 = (bf16[256,512]{1,0:T(8,128)(2,1)S(1)}, bf16[256,512]{1,0:T(8,128)(2,1)S(1)}, u32[]{:S(2)}, u32[]{:S(2)}) collective-permute-start(bf16[256,512]{1,0:T(8,128)(2,1)S(1)} %pad_maximum_fusion.4), channel_id=1, source_target_pairs={{0,2},{1,3},{2,0},{3,1},{4,6},{5,7},{6,4},{7,5},{8,10},{9,11},{10,... | collective-permute-start | bytes 786440 | tf_op jit(solution)/shard_map/ppermute | solution.py:246
  143.6 4.2 %collective-permute-done.25 = bf16[128,512]{1,0:T(8,128)(2,1)S(1)} collective-permute-done((bf16[128,512]{1,0:T(8,128)(2,1)S(1)}, bf16[128,512]{1,0:T(8,128)(2,1)S(1)}, u32[]{:S(2)}, u32[]{:S(2)}) %collective-permute-start.25) | collective-permute-done | bytes 131104 | tf_op jit(solution)/shard_map/ppermute | solution.py:246
  148.6 1.8 %collective-permute-start.24 = (bf16[272,512]{1,0:T(8,128)(2,1)S(1)}, bf16[272,512]{1,0:T(8,128)(2,1)S(1)}, u32[]{:S(2)}, u32[]{:S(2)}) collective-permute-start(bf16[272,512]{1,0:T(8,128)(2,1)S(1)} %pad_maximum_fusion.2), channel_id=1, source_target_pairs={{0,2},{1,3},{2,0},{3,1},{4,6},{5,7},{6,4},{7,5},{8,10},{9,11},{10,... | collective-permute-start | bytes 835592 | tf_op jit(solution)/shard_map/ppermute | solution.py:246
  150.7 5.6 %collective-permute-done.26 = bf16[272,512]{1,0:T(8,128)(2,1)S(1)} collective-permute-done((bf16[272,512]{1,0:T(8,128)(2,1)S(1)}, bf16[272,512]{1,0:T(8,128)(2,1)S(1)}, u32[]{:S(2)}, u32[]{:S(2)}) %collective-permute-start.26) | collective-permute-done | bytes 278560 | tf_op jit(solution)/shard_map/ppermute | solution.py:246
  156.3 1.4 collective-permute-done.24
  (106 shorter events, 28.9 us)
Async XLA Ops:
  0.7 14.0 %collective-permute-start = (bf16[2,256,512]{2,1,0:T(8,128)(2,1)}, bf16[2,256,512]{2,1,0:T(8,128)(2,1)}, u32[]{:S(2)}, u32[]{:S(2)}) collective-permute-start(bf16[2,256,512]{2,1,0:T(8,128)(2,1)} %refs_6_.1), channel_id=1, source_target_pairs={{0,2},{1,3},{2,0},{3,1},{4,6},{5,7},{6,4},{7,5},{8,10},{9,11},{10,... | collective-permute-start | bytes 1572872 | tf_op jit(solution)/shard_map/ppermute | solution.py:246
  2.2 13.7 %collective-permute-start.1 = (bf16[2,256,512]{2,1,0:T(8,128)(2,1)}, bf16[2,256,512]{2,1,0:T(8,128)(2,1)}, u32[]{:S(2)}, u32[]{:S(2)}) collective-permute-start(bf16[2,256,512]{2,1,0:T(8,128)(2,1)} %refs_6_.1), channel_id=1, source_target_pairs={{0,4},{1,5},{2,6},{3,7},{4,0},{5,1},{6,2},{7,3},{8,12},{9,13},{10,... | collective-permute-start | bytes 1572872 | tf_op jit(solution)/shard_map/ppermute | solution.py:246
  3.7 20.7 %collective-permute-start.2 = (bf16[2,256,512]{2,1,0:T(8,128)(2,1)}, bf16[2,256,512]{2,1,0:T(8,128)(2,1)S(1)}, u32[]{:S(2)}, u32[]{:S(2)}) collective-permute-start(bf16[2,256,512]{2,1,0:T(8,128)(2,1)} %refs_6_.1), channel_id=1, source_target_pairs={{0,1},{1,0},{2,3},{3,2},{4,5},{5,4},{6,7},{7,6},{8,9},{9,8},{10,11... | collective-permute-start | bytes 1572872 | tf_op jit(solution)/shard_map/ppermute | solution.py:246
  3.8 26.2 %collective-permute-start.9 = (bf16[2,512,512]{2,1,0:T(8,128)(2,1)}, bf16[2,512,512]{2,1,0:T(8,128)(2,1)S(1)}, u32[]{:S(2)}, u32[]{:S(2)}) collective-permute-start(bf16[2,512,512]{2,1,0:T(8,128)(2,1)} %refs_2_.11), channel_id=1, source_target_pairs={{0,8},{8,0},{16,24},{24,16},{1,9},{9,1},{17,25},{25,17},{2,10},{10... | collective-permute-start | bytes 3145736 | tf_op jit(solution)/shard_map/ppermute | solution.py:246
  11.5 16.3 %copy-start.13 = (s32[2]{0:T(128)S(1)}, s32[2]{0:T(128)}, u32[]{:S(2)}) copy-start(s32[2]{0:T(128)} %param.20) | copy-start | bytes 28
  11.5 16.2 %copy-start.14 = (s32[2]{0:T(128)S(1)}, s32[2]{0:T(128)}, u32[]{:S(2)}) copy-start(s32[2]{0:T(128)} %param.21) | copy-start | bytes 28
  11.5 18.4 %copy-start.4 = (f32[3,512]{1,0:T(4,128)S(1)}, f32[3,512]{1,0:T(4,128)}, u32[]{:S(2)}) copy-start(f32[3,512]{1,0:T(4,128)} %refs_3_.3) | copy-start | bytes 18436
  16.9 7.0 %collective-permute-start.5 = (bf16[256,512]{1,0:T(8,128)(2,1)S(1)}, bf16[256,512]{1,0:T(8,128)(2,1)}, u32[]{:S(2)}, u32[]{:S(2)}) collective-permute-start(bf16[256,512]{1,0:T(8,128)(2,1)S(1)} %slice_bitcast_fusion.5), channel_id=1, source_target_pairs={{0,2},{1,3},{2,0},{3,1},{4,6},{5,7},{6,4},{7,5},{8,10},{9,11},{10,... | collective-permute-start | bytes 786440 | tf_op jit(solution)/shard_map/ppermute | solution.py:246
  19.2 7.0 %collective-permute-start.6 = (bf16[256,512]{1,0:T(8,128)(2,1)}, bf16[256,512]{1,0:T(8,128)(2,1)}, u32[]{:S(2)}, u32[]{:S(2)}) collective-permute-start(bf16[256,512]{1,0:T(8,128)(2,1)} %slice_bitcast_fusion.4), channel_id=1, source_target_pairs={{0,4},{1,5},{2,6},{3,7},{4,0},{5,1},{6,2},{7,3},{8,12},{9,13},{10,... | collective-permute-start | bytes 786440 | tf_op jit(solution)/shard_map/ppermute | solution.py:246
  23.9 3.8 %collective-permute-start.7 = (bf16[256,512]{1,0:T(8,128)(2,1)}, bf16[256,512]{1,0:T(8,128)(2,1)}, u32[]{:S(2)}, u32[]{:S(2)}) collective-permute-start(bf16[256,512]{1,0:T(8,128)(2,1)} %collective-permute-done.5.refs_12_), channel_id=1, source_target_pairs={{0,1},{1,0},{2,3},{3,2},{4,5},{5,4},{6,7},{7,6},{8,9},{9,8},{10,11... | collective-permute-start | bytes 786440 | tf_op jit(solution)/shard_map/ppermute | solution.py:246
  23.9 5.7 %collective-permute-start.3 = (bf16[2,256,512]{2,1,0:T(8,128)(2,1)}, bf16[2,256,512]{2,1,0:T(8,128)(2,1)}, u32[]{:S(2)}, u32[]{:S(2)}) collective-permute-start(bf16[2,256,512]{2,1,0:T(8,128)(2,1)} %collective-permute-done.refs_8_), channel_id=1, source_target_pairs={{0,1},{1,0},{2,3},{3,2},{4,5},{5,4},{6,7},{7,6},{8,9},{9,8},{10,11... | collective-permute-start | bytes 1572872 | tf_op jit(solution)/shard_map/ppermute | solution.py:246
  25.2 4.4 %collective-permute-start.4 = (bf16[2,256,512]{2,1,0:T(8,128)(2,1)}, bf16[2,256,512]{2,1,0:T(8,128)(2,1)}, u32[]{:S(2)}, u32[]{:S(2)}) collective-permute-start(bf16[2,256,512]{2,1,0:T(8,128)(2,1)} %collective-permute-done.1.refs_10_), channel_id=1, source_target_pairs={{0,1},{1,0},{2,3},{3,2},{4,5},{5,4},{6,7},{7,6},{8,9},{9,8},{10,11... | collective-permute-start | bytes 1572872 | tf_op jit(solution)/shard_map/ppermute | solution.py:246
  26.1 36.3 %collective-permute-start.11 = (bf16[2,512,512]{2,1,0:T(8,128)(2,1)S(1)}, bf16[2,512,512]{2,1,0:T(8,128)(2,1)S(1)}, u32[]{:S(2)}, u32[]{:S(2)}) collective-permute-start(bf16[2,512,512]{2,1,0:T(8,128)(2,1)S(1)} %bitcast.74), channel_id=1, source_target_pairs={{0,8},{8,0},{16,24},{24,16},{1,9},{9,1},{17,25},{25,17},{2,10},{10... | collective-permute-start | bytes 3145736 | tf_op jit(solution)/shard_map/ppermute | solution.py:246
  27.7 1.9 %collective-permute-start.8 = (bf16[256,512]{1,0:T(8,128)(2,1)}, bf16[256,512]{1,0:T(8,128)(2,1)}, u32[]{:S(2)}, u32[]{:S(2)}) collective-permute-start(bf16[256,512]{1,0:T(8,128)(2,1)} %collective-permute-done.6.refs_13_), channel_id=1, source_target_pairs={{0,1},{1,0},{2,3},{3,2},{4,5},{5,4},{6,7},{7,6},{8,9},{9,8},{10,11... | collective-permute-start | bytes 786440 | tf_op jit(solution)/shard_map/ppermute | solution.py:246
  31.1 17.9 %copy-start.12 = (f32[1536]{0:T(1024)S(1)}, f32[1536]{0:T(1024)}, u32[]{:S(2)}) copy-start(f32[1536]{0:T(1024)} %param.33) | copy-start | bytes 18436
  46.4 24.9 %collective-permute-start.10 = (bf16[2,256,512]{2,1,0:T(8,128)(2,1)S(1)}, bf16[2,256,512]{2,1,0:T(8,128)(2,1)S(1)}, u32[]{:S(2)}, u32[]{:S(2)}) collective-permute-start(bf16[2,256,512]{2,1,0:T(8,128)(2,1)S(1)} %bitcast.80), channel_id=1, source_target_pairs={{0,24},{8,16},{16,8},{24,0},{1,25},{9,17},{17,9},{25,1},{2,26},{10... | collective-permute-start | bytes 1572872 | tf_op jit(solution)/shard_map/ppermute | solution.py:246
  46.9 39.7 %collective-permute-start.12 = (bf16[2,256,512]{2,1,0:T(8,128)(2,1)}, bf16[2,256,512]{2,1,0:T(8,128)(2,1)S(1)}, u32[]{:S(2)}, u32[]{:S(2)}) collective-permute-start(bf16[2,256,512]{2,1,0:T(8,128)(2,1)} %get-tuple-element.21.refs_4_), channel_id=1, source_target_pairs={{0,8},{8,0},{16,24},{24,16},{1,9},{9,1},{17,25},{25,17},{2,10},{10... | collective-permute-start | bytes 1572872 | tf_op jit(solution)/shard_map/ppermute | solution.py:246
  48.2 38.3 %collective-permute-start.13 = (bf16[2,512,256]{2,1,0:T(8,128)(2,1)S(1)}, bf16[2,512,256]{2,1,0:T(8,128)(2,1)S(1)}, u32[]{:S(2)}, u32[]{:S(2)}) collective-permute-start(bf16[2,512,256]{2,1,0:T(8,128)(2,1)S(1)} %get-tuple-element.31.refs_5_), channel_id=1, source_target_pairs={{0,8},{8,0},{16,24},{24,16},{1,9},{9,1},{17,25},{25,17},{2,10},{10... | collective-permute-start | bytes 1572872 | tf_op jit(solution)/shard_map/ppermute | solution.py:246
  95.7 27.6 %collective-permute-start.16 = (bf16[528,256]{1,0:T(8,128)(2,1)S(1)}, bf16[528,256]{1,0:T(8,128)(2,1)S(1)}, u32[]{:S(2)}, u32[]{:S(2)}) collective-permute-start(bf16[528,256]{1,0:T(8,128)(2,1)S(1)} %get-tuple-element.37.refs_10_), channel_id=1, source_target_pairs={{0,24},{8,16},{16,8},{24,0},{1,25},{9,17},{17,9},{25,1},{2,26},{10... | collective-permute-start | bytes 811016 | tf_op jit(solution)/shard_map/ppermute | solution.py:246
  96.0 27.9 %collective-permute-start.14 = (bf16[528,256]{1,0:T(8,128)(2,1)S(1)}, bf16[528,256]{1,0:T(8,128)(2,1)S(1)}, u32[]{:S(2)}, u32[]{:S(2)}) collective-permute-start(bf16[528,256]{1,0:T(8,128)(2,1)S(1)} %get-tuple-element.34.refs_9_), channel_id=1, source_target_pairs={{0,24},{8,16},{16,8},{24,0},{1,25},{9,17},{17,9},{25,1},{2,26},{10... | collective-permute-start | bytes 811016 | tf_op jit(solution)/shard_map/ppermute | solution.py:246
  97.8 26.2 %copy-start.1 = (bf16[512,4096]{1,0:T(8,128)(2,1)S(1)}, bf16[512,4096]{1,0:T(8,128)(2,1)}, u32[]{:S(2)}) copy-start(bf16[512,4096]{1,0:T(8,128)(2,1)} %refs_4_.1) | copy-start | bytes 12582916
  100.4 22.9 %collective-permute-start.15 = (f32[32,512]{1,0:T(8,128)S(1)}, f32[32,512]{1,0:T(8,128)S(1)}, u32[]{:S(2)}, u32[]{:S(2)}) collective-permute-start(f32[32,512]{1,0:T(8,128)S(1)} %shard_map.210.refs_4_), channel_id=1, source_target_pairs={{0,24},{8,16},{16,8},{24,0},{1,25},{9,17},{17,9},{25,1},{2,26},{10... | collective-permute-start | bytes 196616 | tf_op jit(solution)/shard_map/ppermute | solution.py:246
  128.2 6.6 %collective-permute-start.17 = (bf16[4,256,512]{2,1,0:T(8,128)(2,1)}, bf16[4,256,512]{2,1,0:T(8,128)(2,1)}, u32[]{:S(2)}, u32[]{:S(2)}) collective-permute-start(bf16[4,256,512]{2,1,0:T(8,128)(2,1)} %get-tuple-element.39), channel_id=1, source_target_pairs={{0,1},{1,0},{2,3},{3,2},{4,5},{5,4},{6,7},{7,6},{8,9},{9,8},{10,11... | collective-permute-start | bytes 3145736 | tf_op jit(solution)/shard_map/ppermute | solution.py:246
  132.2 6.3 %collective-permute-start.22 = (bf16[4,272,512]{2,1,0:T(8,128)(2,1)S(1)}, bf16[4,272,512]{2,1,0:T(8,128)(2,1)}, u32[]{:S(2)}, u32[]{:S(2)}) collective-permute-start(bf16[4,272,512]{2,1,0:T(8,128)(2,1)S(1)} %get-tuple-element.42), channel_id=1, source_target_pairs={{0,1},{1,0},{2,3},{3,2},{4,5},{5,4},{6,7},{7,6},{8,9},{9,8},{10,11... | collective-permute-start | bytes 3342344 | tf_op jit(solution)/shard_map/ppermute | solution.py:246
  136.2 5.7 %collective-permute-start.18 = (bf16[128,512]{1,0:T(8,128)(2,1)S(1)}, bf16[128,512]{1,0:T(8,128)(2,1)S(1)}, u32[]{:S(2)}, u32[]{:S(2)}) collective-permute-start(bf16[128,512]{1,0:T(8,128)(2,1)S(1)} %get-tuple-element.52), channel_id=1, source_target_pairs={{0,4},{1,5},{2,6},{3,7},{4,0},{5,1},{6,2},{7,3},{8,12},{9,13},{10,... | collective-permute-start | bytes 393224 | tf_op jit(solution)/shard_map/ppermute | solution.py:246
  138.1 12.3 %collective-permute-start.20 = (bf16[128,512]{1,0:T(8,128)(2,1)S(1)}, bf16[128,512]{1,0:T(8,128)(2,1)S(1)}, u32[]{:S(2)}, u32[]{:S(2)}) collective-permute-start(bf16[128,512]{1,0:T(8,128)(2,1)S(1)} %get-tuple-element.53), channel_id=1, source_target_pairs={{0,2},{1,3},{2,0},{3,1},{4,6},{5,7},{6,4},{7,5},{8,10},{9,11},{10,... | collective-permute-start | bytes 393224 | tf_op jit(solution)/shard_map/ppermute | solution.py:246
  139.9 8.6 %collective-permute-start.23 = (bf16[144,512]{1,0:T(8,128)(2,1)S(1)}, bf16[144,512]{1,0:T(8,128)(2,1)S(1)}, u32[]{:S(2)}, u32[]{:S(2)}) collective-permute-start(bf16[144,512]{1,0:T(8,128)(2,1)S(1)} %slice_bitcast_fusion.6), channel_id=1, source_target_pairs={{0,4},{1,5},{2,6},{3,7},{4,0},{5,1},{6,2},{7,3},{8,12},{9,13},{10,... | collective-permute-start | bytes 442376 | tf_op jit(solution)/shard_map/ppermute | solution.py:246
  141.4 6.4 %collective-permute-start.25 = (bf16[128,512]{1,0:T(8,128)(2,1)S(1)}, bf16[128,512]{1,0:T(8,128)(2,1)S(1)}, u32[]{:S(2)}, u32[]{:S(2)}) collective-permute-start(bf16[128,512]{1,0:T(8,128)(2,1)S(1)} %slice_bitcast_fusion.7), channel_id=1, source_target_pairs={{0,2},{1,3},{2,0},{3,1},{4,6},{5,7},{6,4},{7,5},{8,10},{9,11},{10,... | collective-permute-start | bytes 393224 | tf_op jit(solution)/shard_map/ppermute | solution.py:246
  142.0 18.1 %collective-permute-start.19 = (bf16[256,512]{1,0:T(8,128)(2,1)S(1)}, bf16[256,512]{1,0:T(8,128)(2,1)S(1)}, u32[]{:S(2)}, u32[]{:S(2)}) collective-permute-start(bf16[256,512]{1,0:T(8,128)(2,1)S(1)} %pad_maximum_fusion.4), channel_id=1, source_target_pairs={{0,2},{1,3},{2,0},{3,1},{4,6},{5,7},{6,4},{7,5},{8,10},{9,11},{10,... | collective-permute-start | bytes 786440 | tf_op jit(solution)/shard_map/ppermute | solution.py:246
  147.9 8.4 %collective-permute-start.26 = (bf16[272,512]{1,0:T(8,128)(2,1)S(1)}, bf16[272,512]{1,0:T(8,128)(2,1)S(1)}, u32[]{:S(2)}, u32[]{:S(2)}) collective-permute-start(bf16[272,512]{1,0:T(8,128)(2,1)S(1)} %pad_maximum_fusion.3), channel_id=1, source_target_pairs={{0,4},{1,5},{2,6},{3,7},{4,0},{5,1},{6,2},{7,3},{8,12},{9,13},{10,... | collective-permute-start | bytes 835592 | tf_op jit(solution)/shard_map/ppermute | solution.py:246
  148.6 9.1 %collective-permute-start.24 = (bf16[272,512]{1,0:T(8,128)(2,1)S(1)}, bf16[272,512]{1,0:T(8,128)(2,1)S(1)}, u32[]{:S(2)}, u32[]{:S(2)}) collective-permute-start(bf16[272,512]{1,0:T(8,128)(2,1)S(1)} %pad_maximum_fusion.2), channel_id=1, source_target_pairs={{0,2},{1,3},{2,0},{3,1},{4,6},{5,7},{6,4},{7,5},{8,10},{9,11},{10,... | collective-permute-start | bytes 835592 | tf_op jit(solution)/shard_map/ppermute | solution.py:246
  150.5 9.6 %collective-permute-start.21 = (bf16[256,512]{1,0:T(8,128)(2,1)S(1)}, bf16[256,512]{1,0:T(8,128)(2,1)S(1)}, u32[]{:S(2)}, u32[]{:S(2)}) collective-permute-start(bf16[256,512]{1,0:T(8,128)(2,1)S(1)} %pad_maximum_fusion.5), channel_id=1, source_target_pairs={{0,4},{1,5},{2,6},{3,7},{4,0},{5,1},{6,2},{7,3},{8,12},{9,13},{10,... | collective-permute-start | bytes 786440 | tf_op jit(solution)/shard_map/ppermute | solution.py:246
  (10 other events, 99.4 us)
where the time goes:
time: 163 us; the launch traced here: 162 us
  Pallas kernels  66.2 us (41%)
  waiting for transfers between devices  50.4 us (31%)
  starting transfers between devices  22.9 us (14%)
  other arithmetic  13.5 us (8%)
  local copies, waits for them, and re-layouts  7.96 us (5%)
    pallas_call x13, Pallas kernels, call(): pl.pallas_call(run, out_shape=outs, in_specs=[pl.BlockSpec(memory_space=p...  66.2 us
    ppermute x27, waiting for transfers between devices, hop(): return lax.ppermute(value, axis, pairs)  50.4 us
    ppermute x27, starting transfers between devices, hop(): return lax.ppermute(value, axis, pairs)  22.9 us
  transfers between devices with their start and end apart: 27, of which 12 were waited for; matrix products, arithmetic and copies ran while one was open for 11% of the time, Pallas kernels for 33%

commit v1 on v0

--- a/solution.py
+++ b/solution.py
@@ -503,8 +503,8 @@
             source,
             kc.at[seq],
             vc.at[seq],
-            kn.at[seq],
-            vn.at[seq],
+            kn,
+            vn,
             *limits(sc, seq, rank ^ 1, asker, pre, rows),
         )
         earlier = unpack_logs(before[pl.ds(cols, LSE), :])
@@ -522,7 +522,7 @@
 
 def attend_second(scal, seq, q, q_far, kv, mine, mine_far, after):
     pre, cols = kv[0].shape[1:]
-    rows = kv[2].shape[1]
+    rows = kv[2].shape[0]
     return call(
         functools.partial(second_body, seq, rows, pre),
         scal,
@@ -534,7 +534,7 @@
 
 def dec_body(seqs, rows, pre, sc, q, kc, vc, kn, vn, *refs):
     far, out = refs[:-1], refs[-1]
-    far = [[a.at[s] for a in far] for s in range(seqs)]
+    far = [(far[0].at[s], far[1].at[s], far[2 + 2 * s], far[3 + 2 * s]) for s in range(seqs)]
     rank = sc[RANK]
     row = lax.broadcasted_iota(jnp.int32, (DEC, 1), 0)
     for at in head_slices(kc.shape[2]):
@@ -800,7 +800,10 @@
     )
     q_far = hop(q[: seqs * rows].reshape(seqs, rows, -1), "ctx", across)
     kv = (key_cache, values_t, new_keys, new_values_t)
-    far_kv = (far_k, far_v, hop(new_keys, "ctx", mate), hop(new_values_t, "ctx", mate))
+    pairs = [
+        (far_k, far_v, hop(new_keys[s], "ctx", mate), hop(new_values_t[s], "ctx", mate))
+        for s in range(seqs)
+    ]
 
     up = up_proj(scal, mlp_in, up_weight, up_bias[None, :], [])
     own, far, last = [], [], [up, far_v]
@@ -810,14 +813,16 @@
     for s in range(seqs):
         far.append(attend_one(far_body, scal, s, q_far, kv, last))
         last = [far[s]]
-    mlp = down_proj(scal, up, down_weight, last)
-    last = [mlp]
+    last.append(pairs[1][2])
     ends = []
     for s in range(seqs):
-        mine, back = attend_second(scal, s, q, q_far, far_kv, own[s], far[s], last)
+        mine, back = attend_second(scal, s, q, q_far, pairs[s], own[s], far[s], last)
         last = [back]
         ends.append((mine, hop(back, "ctx", across)))
-    dec = attend_dec(scal, q, kv, far_kv, last)
+        if s == 0:
+            mlp = down_proj(scal, up, down_weight, [back, pairs[1][3]])
+            last = [mlp]
+    dec = attend_dec(scal, q, kv, [*pairs[0], *pairs[1][2:]], last)
     dec_far = hop(dec, "ctx", across)
     attn_dec = decode_attn(scal, q, k_dec, v_dec, [dec, dec_far], [ends[-1][1]])
     last = attn_dec

time: 163 us -> 168 us (1.031)
  starting transfers between devices: 22.9 us -> 26.6 us
  Pallas kernels: 66.2 us -> 68.6 us
    ppermute x27 -> x29, starting transfers between devices: 22.9 us -> 26.6 us  [hop(): return lax.ppermute(value, axis, pairs)]
    pallas_call x13, Pallas kernels: 66.2 us -> 68.6 us  [call(): pl.pallas_call(run, out_shape=outs, in_specs=[pl.BlockSpec(memory_space=p...]
    ppermute x27 -> x29, waiting for transfers between devices: 50.4 us -> 50.5 us  [hop(): return lax.ppermute(value, axis, pairs)]
  transfers between devices with their start and end apart: 27 -> 29, of which waited for: 12 -> 13; matrix products, arithmetic and copies ran while one was open for 11% -> 10% of each run, Pallas kernels for 33% -> 29%
where the time goes in v1:
time: 168 us; the launch traced here: 167 us
  Pallas kernels  68.6 us (41%)
  waiting for transfers between devices  50.5 us (30%)
  starting transfers between devices  26.6 us (16%)
  other arithmetic  12.7 us (8%)
  local copies, waits for them, and re-layouts  7.64 us (5%)
    pallas_call x13, Pallas kernels, call(): pl.pallas_call(run, out_shape=outs, in_specs=[pl.BlockSpec(memory_space=p...  68.6 us
    ppermute x29, waiting for transfers between devices, hop(): return lax.ppermute(value, axis, pairs)  50.5 us
    ppermute x29, starting transfers between devices, hop(): return lax.ppermute(value, axis, pairs)  26.6 us
  transfers between devices with their start and end apart: 29, of which 13 were waited for; matrix products, arithmetic and copies ran while one was open for 10% of the time, Pallas kernels for 29%

profile of v1, /device:TPU:16, one launch (start us, length us, event | category | flops | bytes accessed | tf_op | source)
XLA Modules:
  0.0 167.3 jit_solution(8209013148336584594)
XLA Ops:
  0.7 1.6 collective-permute-start
  2.2 1.5 collective-permute-start.1
  3.8 1.6 collective-permute-start.9
  10.7 3.9 %collective-permute-done.refs_8_ = bf16[2,256,512]{2,1,0:T(8,128)(2,1)S(1)} collective-permute-done((bf16[2,256,512]{2,1,0:T(8,128)(2,1)}, bf16[2,256,512]{2,1,0:T(8,128)(2,1)S(1)}, u32[]{:S(2)}, u32[]{:S(2)}) %collective-permute-start) | collective-permute-done | bytes 524320 | tf_op jit(solution)/shard_map/ppermute | solution.py:246
  17.9 1.5 collective-permute-start.6
  19.4 1.5 copy.22
  20.9 1.6 collective-permute-start.11
  26.2 1.7 collective-permute-done.8.refs_15_
  27.9 2.1 %collective-permute-done.9.refs_16_.refs_3_.refs_6_ = bf16[2,512,512]{2,1,0:T(8,128)(2,1)} collective-permute-done((bf16[2,512,512]{2,1,0:T(8,128)(2,1)}, bf16[2,512,512]{2,1,0:T(8,128)(2,1)}, u32[]{:S(2)}, u32[]{:S(2)}) %collective-permute-start.9) | collective-permute-done | bytes 1048608 | tf_op jit(solution)/shard_map/ppermute | solution.py:246
  30.0 15.4 %shard_map.201 = (bf16[528,512]{1,0:T(8,128)(2,1)S(1)}, bf16[2,256,512]{2,1,0:T(8,128)(2,1)}, bf16[2,256,512]{2,1,0:T(8,128)(2,1)}, bf16[2,512,256]{2,1,0:T(8,12...) custom-call(s32[34]{0:T(128)S(1)} %pad_add_fusion.1.refs_0_, ...), custom_call_target="tpu_custom_call" | custom-call | tf_op jit(solution)/shard_map/pallas_call | solution.py:256
  50.6 11.8 %collective-permute-done.11.refs_7_.refs_4_ = bf16[2,512,512]{2,1,0:T(8,128)(2,1)S(1)} collective-permute-done((bf16[2,512,512]{2,1,0:T(8,128)(2,1)S(1)}, bf16[2,512,512]{2,1,0:T(8,128)(2,1)S(1)}, u32[]{:S(2)}, u32[]{:S(2)}) %collective-permute-start.11) | collective-permute-done | bytes 1048608 | tf_op jit(solution)/shard_map/ppermute | solution.py:246
  62.4 2.8 %collective-permute-start.16 = (bf16[512,256]{1,0:T(8,128)(2,1)S(1)}, bf16[512,256]{1,0:T(8,128)(2,1)S(1)}, u32[]{:S(2)}, u32[]{:S(2)}) collective-permute-start(bf16[512,256]{1,0:T(8,128)(2,1)S(1)} %get-tuple-element.53), channel_id=1, source_target_pairs={{0,8},{8,0},{16,24},{24,16},{1,9},{9,1},{17,25},{25,17},{2,10},{10... | collective-permute-start | bytes 786440 | tf_op jit(solution)/shard_map/ppermute | solution.py:246
  65.2 10.4 %shard_map.202.refs_6_.refs_1_ = bf16[528,1536]{1,0:T(8,128)(2,1)S(1)} custom-call(s32[34]{0:T(128)S(1)} %pad_add_fusion.1.refs_0_, bf16[528,4096]{1,0:T(8,128)(2,1)S(1)} %get-tuple-element.32.refs_1_, f32[1,1536]{1,0:T(1,128)S(1)} %broadcast_in_dim.52.refs_2_, bf16[4096,1536]{1,0:T(8,128)(2,1)} %refs_3_.4), custom_call_target="tpu_custom_call" | custom-call | tf_op jit(solution)/shard_map/pallas_call | solution.py:256
  75.7 2.6 %shard_map.203.refs_6_.refs_7_ = bf16[528,256]{1,0:T(8,128)(2,1)S(1)} custom-call(s32[34]{0:T(128)S(1)} %pad_add_fusion.1.refs_0_, bf16[528,512]{1,0:T(8,128)(2,1)S(1)} %get-tuple-element.29.refs_1_, bf16[2,512,512]{2,1,0:T(8,128)(2,1)S(1)} %copy-done, bf16[2,512,512]{2,1,0:T(8,128)(2,1)S(1)} %bitcast.83, bf16[2,256,512]{2,1,0:T(8,128)(2,1)S(1)} %copy-done.1, ...), custom_call_target="tpu_custom_call" | custom-call | tf_op jit(solution)/shard_map/pallas_call | solution.py:256
  78.3 2.6 %shard_map.204.refs_6_.refs_7_ = bf16[528,256]{1,0:T(8,128)(2,1)S(1)} custom-call(s32[34]{0:T(128)S(1)} %pad_add_fusion.1.refs_0_, bf16[528,512]{1,0:T(8,128)(2,1)S(1)} %get-tuple-element.29.refs_1_, bf16[2,512,512]{2,1,0:T(8,128)(2,1)S(1)} %copy-done, bf16[2,512,512]{2,1,0:T(8,128)(2,1)S(1)} %bitcast.84, bf16[2,256,512]{2,1,0:T(8,128)(2,1)S(1)} %copy-done.1, ...), custom_call_target="tpu_custom_call" | custom-call | tf_op jit(solution)/shard_map/pallas_call | solution.py:256
  81.0 2.6 %shard_map.205.refs_6_.refs_8_ = bf16[528,256]{1,0:T(8,128)(2,1)S(1)} custom-call(s32[34]{0:T(128)S(1)} %pad_add_fusion.1.refs_0_, bf16[2,256,512]{2,1,0:T(8,128)(2,1)S(1)} %collective-permute-done.10.refs_1_.refs_2_, bf16[2,512,512]{2,1,0:T(8,128)(2,1)S(1)} %copy-done, bf16[2,512,512]{2,1,0:T(8,128)(2,1)S(1)} %bitcast.85, ...), custom_call_target="tpu_custom_call" | custom-call | tf_op jit(solution)/shard_map/pallas_call | solution.py:256
  83.6 2.6 %shard_map.206.refs_9_.refs_8_ = bf16[528,256]{1,0:T(8,128)(2,1)S(1)} custom-call(s32[34]{0:T(128)S(1)} %pad_add_fusion.1.refs_0_, bf16[2,256,512]{2,1,0:T(8,128)(2,1)S(1)} %collective-permute-done.10.refs_1_.refs_2_, bf16[2,512,512]{2,1,0:T(8,128)(2,1)S(1)} %copy-done, bf16[2,512,512]{2,1,0:T(8,128)(2,1)S(1)} %bitcast.86, ...), custom_call_target="tpu_custom_call" | custom-call | tf_op jit(solution)/shard_map/pallas_call | solution.py:256
  86.3 5.2 %shard_map.207 = (bf16[528,256]{1,0:T(8,128)(2,1)S(1)}, bf16[528,256]{1,0:T(8,128)(2,1)S(1)}) custom-call(s32[34]{0:T(128)S(1)} %pad_add_fusion.1.refs_0_, bf16[528,512]{1,0:T(8,128)(2,1)S(1)} %get-tuple-element.29.refs_1_, bf16[2,256,512]{2,1,0:T(8,128)(2,1)S(1)} %collective-permute-done.10.refs_1_.refs_2_, ...), custom_call_target="tpu_custom_call" | custom-call | tf_op jit(solution)/shard_map/pallas_call | solution.py:256
  91.5 10.2 %shard_map.208.refs_9_.refs_4_.refs_5_ = bf16[528,4096]{1,0:T(8,128)(2,1)S(1)} custom-call(s32[34]{0:T(128)S(1)} %pad_add_fusion.1.refs_0_, bf16[528,1536]{1,0:T(8,128)(2,1)S(1)} %shard_map.202.refs_6_.refs_1_, bf16[1536,4096]{1,0:T(8,128)(2,1)} %refs_2_.10, bf16[528,256]{1,0:T(8,128)(2,1)S(1)} %get-tuple-element.34.refs_3_, ...), custom_call_target="tpu_custom_call" | custom-call | tf_op jit(solution)/shard_map/pallas_call | solution.py:256
  101.6 5.2 %shard_map.209 = (bf16[528,256]{1,0:T(8,128)(2,1)S(1)}, bf16[528,256]{1,0:T(8,128)(2,1)S(1)}) custom-call(s32[34]{0:T(128)S(1)} %pad_add_fusion.1.refs_0_, bf16[528,512]{1,0:T(8,128)(2,1)S(1)} %get-tuple-element.29.refs_1_, bf16[2,256,512]{2,1,0:T(8,128)(2,1)S(1)} %collective-permute-done.10.refs_1_.refs_2_, ...), custom_call_target="tpu_custom_call" | custom-call | tf_op jit(solution)/shard_map/pallas_call | solution.py:256
  106.9 2.0 %collective-permute-start.15 = (bf16[528,256]{1,0:T(8,128)(2,1)S(1)}, bf16[528,256]{1,0:T(8,128)(2,1)S(1)}, u32[]{:S(2)}, u32[]{:S(2)}) collective-permute-start(bf16[528,256]{1,0:T(8,128)(2,1)S(1)} %get-tuple-element.34.refs_3_), channel_id=1, source_target_pairs={{0,24},{8,16},{16,8},{24,0},{1,25},{9,17},{17,9},{25,1},{2,26},{10... | collective-permute-start | bytes 811016 | tf_op jit(solution)/shard_map/ppermute | solution.py:246
  108.9 3.5 %shard_map.210.refs_4_ = f32[32,512]{1,0:T(8,128)S(1)} custom-call(s32[34]{0:T(128)S(1)} %pad_add_fusion.1.refs_0_, bf16[528,512]{1,0:T(8,128)(2,1)S(1)} %get-tuple-element.29.refs_1_, bf16[2,512,512]{2,1,0:T(8,128)(2,1)S(1)} %copy-done, bf16[2,512,512]{2,1,0:T(8,128)(2,1)S(1)} %bitcast.87, bf16[2,256,512]{2,1,0:T(8,128)(2,1)S(1)} %copy-done.1, ...), custom_call_target="tpu_custom_call" | custom-call | tf_op jit(solution)/shard_map/pallas_call | solution.py:256
  112.5 17.0 %collective-permute-done.17.refs_5_ = f32[32,512]{1,0:T(8,128)S(1)} collective-permute-done((f32[32,512]{1,0:T(8,128)S(1)}, f32[32,512]{1,0:T(8,128)S(1)}, u32[]{:S(2)}, u32[]{:S(2)}) %collective-permute-start.17) | collective-permute-done | bytes 65568 | tf_op jit(solution)/shard_map/ppermute | solution.py:246
  130.2 4.3 %shard_map.212 = (bf16[4,256,512]{2,1,0:T(8,128)(2,1)}, bf16[4,256,512]{2,1,0:T(8,128)(2,1)S(1)}) custom-call(s32[34]{0:T(128)S(1)} %pad_add_fusion.1.refs_0_, bf16[528,256]{1,0:T(8,128)(2,1)S(1)} %get-tuple-element.33.refs_1_, bf16[528,256]{1,0:T(8,128)(2,1)S(1)} %collective-permute-done.15.refs_2_, bf16[512,4096]{1,0:T(8,128)(2,1)S(1)} %copy-done.2, ...), custom_call_target="tpu_custom_call" | custom-call | tf_op jit(solution)/shard_map/pallas_call | solution.py:256
  135.0 3.4 %shard_map.213 = (bf16[4,272,512]{2,1,0:T(8,128)(2,1)S(1)}, bf16[4,272,512]{2,1,0:T(8,128)(2,1)S(1)}) custom-call(s32[34]{0:T(128)S(1)} %pad_add_fusion.1.refs_0_, bf16[528,256]{1,0:T(8,128)(2,1)S(1)} %get-tuple-element.40.refs_1_, bf16[528,256]{1,0:T(8,128)(2,1)S(1)} %collective-permute-done.18.refs_6_.refs_2_, ...), custom_call_target="tpu_custom_call" | custom-call | tf_op jit(solution)/shard_map/pallas_call | solution.py:256
  145.0 1.5 collective-permute-start.25
  146.5 1.5 collective-permute-start.27
  148.8 4.1 %collective-permute-done.27 = bf16[128,512]{1,0:T(8,128)(2,1)S(1)} collective-permute-done((bf16[128,512]{1,0:T(8,128)(2,1)S(1)}, bf16[128,512]{1,0:T(8,128)(2,1)S(1)}, u32[]{:S(2)}, u32[]{:S(2)}) %collective-permute-start.27) | collective-permute-done | bytes 131104 | tf_op jit(solution)/shard_map/ppermute | solution.py:246
  153.7 1.6 collective-permute-start.26
  155.4 1.6 collective-permute-start.23
  156.9 4.4 %collective-permute-done.28 = bf16[272,512]{1,0:T(8,128)(2,1)S(1)} collective-permute-done((bf16[272,512]{1,0:T(8,128)(2,1)S(1)}, bf16[272,512]{1,0:T(8,128)(2,1)S(1)}, u32[]{:S(2)}, u32[]{:S(2)}) %collective-permute-start.28) | collective-permute-done | bytes 278560 | tf_op jit(solution)/shard_map/ppermute | solution.py:246
  161.3 1.4 collective-permute-done.26
  (114 shorter events, 31.3 us)
Async XLA Ops:
  0.7 13.9 %collective-permute-start = (bf16[2,256,512]{2,1,0:T(8,128)(2,1)}, bf16[2,256,512]{2,1,0:T(8,128)(2,1)S(1)}, u32[]{:S(2)}, u32[]{:S(2)}) collective-permute-start(bf16[2,256,512]{2,1,0:T(8,128)(2,1)} %refs_6_.1), channel_id=1, source_target_pairs={{0,2},{1,3},{2,0},{3,1},{4,6},{5,7},{6,4},{7,5},{8,10},{9,11},{10,... | collective-permute-start | bytes 1572872 | tf_op jit(solution)/shard_map/ppermute | solution.py:246
  2.2 13.6 %collective-permute-start.1 = (bf16[2,256,512]{2,1,0:T(8,128)(2,1)}, bf16[2,256,512]{2,1,0:T(8,128)(2,1)S(1)}, u32[]{:S(2)}, u32[]{:S(2)}) collective-permute-start(bf16[2,256,512]{2,1,0:T(8,128)(2,1)} %refs_6_.1), channel_id=1, source_target_pairs={{0,4},{1,5},{2,6},{3,7},{4,0},{5,1},{6,2},{7,3},{8,12},{9,13},{10,... | collective-permute-start | bytes 1572872 | tf_op jit(solution)/shard_map/ppermute | solution.py:246
  3.7 20.0 %collective-permute-start.2 = (bf16[2,256,512]{2,1,0:T(8,128)(2,1)}, bf16[2,256,512]{2,1,0:T(8,128)(2,1)}, u32[]{:S(2)}, u32[]{:S(2)}) collective-permute-start(bf16[2,256,512]{2,1,0:T(8,128)(2,1)} %refs_6_.1), channel_id=1, source_target_pairs={{0,1},{1,0},{2,3},{3,2},{4,5},{5,4},{6,7},{7,6},{8,9},{9,8},{10,11... | collective-permute-start | bytes 1572872 | tf_op jit(solution)/shard_map/ppermute | solution.py:246
  3.8 26.3 %collective-permute-start.9 = (bf16[2,512,512]{2,1,0:T(8,128)(2,1)}, bf16[2,512,512]{2,1,0:T(8,128)(2,1)}, u32[]{:S(2)}, u32[]{:S(2)}) collective-permute-start(bf16[2,512,512]{2,1,0:T(8,128)(2,1)} %refs_2_.11), channel_id=1, source_target_pairs={{0,8},{8,0},{16,24},{24,16},{1,9},{9,1},{17,25},{25,17},{2,10},{10... | collective-permute-start | bytes 3145736 | tf_op jit(solution)/shard_map/ppermute | solution.py:246
  10.6 19.4 %copy-start.3 = (f32[3,512]{1,0:T(4,128)S(1)}, f32[3,512]{1,0:T(4,128)}, u32[]{:S(2)}) copy-start(f32[3,512]{1,0:T(4,128)} %refs_3_.3) | copy-start | bytes 18436
  16.6 7.2 %collective-permute-start.5 = (bf16[256,512]{1,0:T(8,128)(2,1)}, bf16[256,512]{1,0:T(8,128)(2,1)S(1)}, u32[]{:S(2)}, u32[]{:S(2)}) collective-permute-start(bf16[256,512]{1,0:T(8,128)(2,1)} %slice_bitcast_fusion.9), channel_id=1, source_target_pairs={{0,2},{1,3},{2,0},{3,1},{4,6},{5,7},{6,4},{7,5},{8,10},{9,11},{10,... | collective-permute-start | bytes 786440 | tf_op jit(solution)/shard_map/ppermute | solution.py:246
  17.9 7.1 %collective-permute-start.6 = (bf16[256,512]{1,0:T(8,128)(2,1)}, bf16[256,512]{1,0:T(8,128)(2,1)}, u32[]{:S(2)}, u32[]{:S(2)}) collective-permute-start(bf16[256,512]{1,0:T(8,128)(2,1)} %slice_bitcast_fusion.8), channel_id=1, source_target_pairs={{0,4},{1,5},{2,6},{3,7},{4,0},{5,1},{6,2},{7,3},{8,12},{9,13},{10,... | collective-permute-start | bytes 786440 | tf_op jit(solution)/shard_map/ppermute | solution.py:246
  20.9 41.5 %collective-permute-start.11 = (bf16[2,512,512]{2,1,0:T(8,128)(2,1)S(1)}, bf16[2,512,512]{2,1,0:T(8,128)(2,1)S(1)}, u32[]{:S(2)}, u32[]{:S(2)}) collective-permute-start(bf16[2,512,512]{2,1,0:T(8,128)(2,1)S(1)} %bitcast.82), channel_id=1, source_target_pairs={{0,8},{8,0},{16,24},{24,16},{1,9},{9,1},{17,25},{25,17},{2,10},{10... | collective-permute-start | bytes 3145736 | tf_op jit(solution)/shard_map/ppermute | solution.py:246
  23.8 1.5 collective-permute-start.7
  23.8 4.1 %collective-permute-start.3 = (bf16[2,256,512]{2,1,0:T(8,128)(2,1)}, bf16[2,256,512]{2,1,0:T(8,128)(2,1)}, u32[]{:S(2)}, u32[]{:S(2)}) collective-permute-start(bf16[2,256,512]{2,1,0:T(8,128)(2,1)} %copy-done.5), channel_id=1, source_target_pairs={{0,1},{1,0},{2,3},{3,2},{4,5},{5,4},{6,7},{7,6},{8,9},{9,8},{10,11... | collective-permute-start | bytes 1572872 | tf_op jit(solution)/shard_map/ppermute | solution.py:246
  24.9 3.0 %collective-permute-start.4 = (bf16[2,256,512]{2,1,0:T(8,128)(2,1)}, bf16[2,256,512]{2,1,0:T(8,128)(2,1)}, u32[]{:S(2)}, u32[]{:S(2)}) collective-permute-start(bf16[2,256,512]{2,1,0:T(8,128)(2,1)} %copy-done.6), channel_id=1, source_target_pairs={{0,1},{1,0},{2,3},{3,2},{4,5},{5,4},{6,7},{7,6},{8,9},{9,8},{10,11... | collective-permute-start | bytes 1572872 | tf_op jit(solution)/shard_map/ppermute | solution.py:246
  26.0 1.9 %collective-permute-start.8 = (bf16[256,512]{1,0:T(8,128)(2,1)}, bf16[256,512]{1,0:T(8,128)(2,1)}, u32[]{:S(2)}, u32[]{:S(2)}) collective-permute-start(bf16[256,512]{1,0:T(8,128)(2,1)} %collective-permute-done.6.refs_13_), channel_id=1, source_target_pairs={{0,1},{1,0},{2,3},{3,2},{4,5},{5,4},{6,7},{7,6},{8,9},{9,8},{10,11... | collective-permute-start | bytes 786440 | tf_op jit(solution)/shard_map/ppermute | solution.py:246
  45.4 19.8 %copy-start.13 = (f32[1536]{0:T(1024)S(1)}, f32[1536]{0:T(1024)}, u32[]{:S(2)}) copy-start(f32[1536]{0:T(1024)} %param.33) | copy-start | bytes 18436
  45.5 35.5 %collective-permute-start.10 = (bf16[2,256,512]{2,1,0:T(8,128)(2,1)S(1)}, bf16[2,256,512]{2,1,0:T(8,128)(2,1)S(1)}, u32[]{:S(2)}, u32[]{:S(2)}) collective-permute-start(bf16[2,256,512]{2,1,0:T(8,128)(2,1)S(1)} %bitcast.88), channel_id=1, source_target_pairs={{0,24},{8,16},{16,8},{24,0},{1,25},{9,17},{17,9},{25,1},{2,26},{10... | collective-permute-start | bytes 1572872 | tf_op jit(solution)/shard_map/ppermute | solution.py:246
  47.0 39.2 %collective-permute-start.12 = (bf16[256,512]{1,0:T(8,128)(2,1)S(1)}, bf16[256,512]{1,0:T(8,128)(2,1)S(1)}, u32[]{:S(2)}, u32[]{:S(2)}) collective-permute-start(bf16[256,512]{1,0:T(8,128)(2,1)S(1)} %get-tuple-element.54), channel_id=1, source_target_pairs={{0,8},{8,0},{16,24},{24,16},{1,9},{9,1},{17,25},{25,17},{2,10},{10... | collective-permute-start | bytes 786440 | tf_op jit(solution)/shard_map/ppermute | solution.py:246
  48.5 37.8 %collective-permute-start.13 = (bf16[512,256]{1,0:T(8,128)(2,1)S(1)}, bf16[512,256]{1,0:T(8,128)(2,1)S(1)}, u32[]{:S(2)}, u32[]{:S(2)}) collective-permute-start(bf16[512,256]{1,0:T(8,128)(2,1)S(1)} %get-tuple-element.52), channel_id=1, source_target_pairs={{0,8},{8,0},{16,24},{24,16},{1,9},{9,1},{17,25},{25,17},{2,10},{10... | collective-permute-start | bytes 786440 | tf_op jit(solution)/shard_map/ppermute | solution.py:246
  49.2 37.0 %collective-permute-start.14 = (bf16[256,512]{1,0:T(8,128)(2,1)S(1)}, bf16[256,512]{1,0:T(8,128)(2,1)S(1)}, u32[]{:S(2)}, u32[]{:S(2)}) collective-permute-start(bf16[256,512]{1,0:T(8,128)(2,1)S(1)} %get-tuple-element.55), channel_id=1, source_target_pairs={{0,8},{8,0},{16,24},{24,16},{1,9},{9,1},{17,25},{25,17},{2,10},{10... | collective-permute-start | bytes 786440 | tf_op jit(solution)/shard_map/ppermute | solution.py:246
  62.4 29.0 %collective-permute-start.16 = (bf16[512,256]{1,0:T(8,128)(2,1)S(1)}, bf16[512,256]{1,0:T(8,128)(2,1)S(1)}, u32[]{:S(2)}, u32[]{:S(2)}) collective-permute-start(bf16[512,256]{1,0:T(8,128)(2,1)S(1)} %get-tuple-element.53), channel_id=1, source_target_pairs={{0,8},{8,0},{16,24},{24,16},{1,9},{9,1},{17,25},{25,17},{2,10},{10... | collective-permute-start | bytes 786440 | tf_op jit(solution)/shard_map/ppermute | solution.py:246
  106.8 22.7 %collective-permute-start.18 = (bf16[528,256]{1,0:T(8,128)(2,1)S(1)}, bf16[528,256]{1,0:T(8,128)(2,1)S(1)}, u32[]{:S(2)}, u32[]{:S(2)}) collective-permute-start(bf16[528,256]{1,0:T(8,128)(2,1)S(1)} %get-tuple-element.37.refs_12_), channel_id=1, source_target_pairs={{0,24},{8,16},{16,8},{24,0},{1,25},{9,17},{17,9},{25,1},{2,26},{10... | collective-permute-start | bytes 811016 | tf_op jit(solution)/shard_map/ppermute | solution.py:246
  106.9 23.3 %collective-permute-start.15 = (bf16[528,256]{1,0:T(8,128)(2,1)S(1)}, bf16[528,256]{1,0:T(8,128)(2,1)S(1)}, u32[]{:S(2)}, u32[]{:S(2)}) collective-permute-start(bf16[528,256]{1,0:T(8,128)(2,1)S(1)} %get-tuple-element.34.refs_3_), channel_id=1, source_target_pairs={{0,24},{8,16},{16,8},{24,0},{1,25},{9,17},{17,9},{25,1},{2,26},{10... | collective-permute-start | bytes 811016 | tf_op jit(solution)/shard_map/ppermute | solution.py:246
  108.9 21.3 %copy-start.2 = (bf16[512,4096]{1,0:T(8,128)(2,1)S(1)}, bf16[512,4096]{1,0:T(8,128)(2,1)}, u32[]{:S(2)}) copy-start(bf16[512,4096]{1,0:T(8,128)(2,1)} %refs_4_.1) | copy-start | bytes 12582916
  112.4 17.1 %collective-permute-start.17 = (f32[32,512]{1,0:T(8,128)S(1)}, f32[32,512]{1,0:T(8,128)S(1)}, u32[]{:S(2)}, u32[]{:S(2)}) collective-permute-start(f32[32,512]{1,0:T(8,128)S(1)} %shard_map.210.refs_4_), channel_id=1, source_target_pairs={{0,24},{8,16},{16,8},{24,0},{1,25},{9,17},{17,9},{25,1},{2,26},{10... | collective-permute-start | bytes 196616 | tf_op jit(solution)/shard_map/ppermute | solution.py:246
  134.5 6.6 %collective-permute-start.19 = (bf16[4,256,512]{2,1,0:T(8,128)(2,1)}, bf16[4,256,512]{2,1,0:T(8,128)(2,1)}, u32[]{:S(2)}, u32[]{:S(2)}) collective-permute-start(bf16[4,256,512]{2,1,0:T(8,128)(2,1)} %get-tuple-element.39), channel_id=1, source_target_pairs={{0,1},{1,0},{2,3},{3,2},{4,5},{5,4},{6,7},{7,6},{8,9},{9,8},{10,11... | collective-permute-start | bytes 3145736 | tf_op jit(solution)/shard_map/ppermute | solution.py:246
  138.4 5.2 %collective-permute-start.24 = (bf16[4,272,512]{2,1,0:T(8,128)(2,1)S(1)}, bf16[4,272,512]{2,1,0:T(8,128)(2,1)}, u32[]{:S(2)}, u32[]{:S(2)}) collective-permute-start(bf16[4,272,512]{2,1,0:T(8,128)(2,1)S(1)} %get-tuple-element.42), channel_id=1, source_target_pairs={{0,1},{1,0},{2,3},{3,2},{4,5},{5,4},{6,7},{7,6},{8,9},{9,8},{10,11... | collective-permute-start | bytes 3342344 | tf_op jit(solution)/shard_map/ppermute | solution.py:246
  142.4 6.2 %collective-permute-start.20 = (bf16[128,512]{1,0:T(8,128)(2,1)S(1)}, bf16[128,512]{1,0:T(8,128)(2,1)S(1)}, u32[]{:S(2)}, u32[]{:S(2)}) collective-permute-start(bf16[128,512]{1,0:T(8,128)(2,1)S(1)} %get-tuple-element.56), channel_id=1, source_target_pairs={{0,4},{1,5},{2,6},{3,7},{4,0},{5,1},{6,2},{7,3},{8,12},{9,13},{10,... | collective-permute-start | bytes 393224 | tf_op jit(solution)/shard_map/ppermute | solution.py:246
  143.0 12.3 %collective-permute-start.22 = (bf16[128,512]{1,0:T(8,128)(2,1)S(1)}, bf16[128,512]{1,0:T(8,128)(2,1)S(1)}, u32[]{:S(2)}, u32[]{:S(2)}) collective-permute-start(bf16[128,512]{1,0:T(8,128)(2,1)S(1)} %get-tuple-element.57), channel_id=1, source_target_pairs={{0,2},{1,3},{2,0},{3,1},{4,6},{5,7},{6,4},{7,5},{8,10},{9,11},{10,... | collective-permute-start | bytes 393224 | tf_op jit(solution)/shard_map/ppermute | solution.py:246
  145.0 8.7 %collective-permute-start.25 = (bf16[144,512]{1,0:T(8,128)(2,1)S(1)}, bf16[144,512]{1,0:T(8,128)(2,1)S(1)}, u32[]{:S(2)}, u32[]{:S(2)}) collective-permute-start(bf16[144,512]{1,0:T(8,128)(2,1)S(1)} %slice_bitcast_fusion.10), channel_id=1, source_target_pairs={{0,4},{1,5},{2,6},{3,7},{4,0},{5,1},{6,2},{7,3},{8,12},{9,13},{10,... | collective-permute-start | bytes 442376 | tf_op jit(solution)/shard_map/ppermute | solution.py:246
  146.5 6.4 %collective-permute-start.27 = (bf16[128,512]{1,0:T(8,128)(2,1)S(1)}, bf16[128,512]{1,0:T(8,128)(2,1)S(1)}, u32[]{:S(2)}, u32[]{:S(2)}) collective-permute-start(bf16[128,512]{1,0:T(8,128)(2,1)S(1)} %slice_bitcast_fusion.11), channel_id=1, source_target_pairs={{0,2},{1,3},{2,0},{3,1},{4,6},{5,7},{6,4},{7,5},{8,10},{9,11},{10,... | collective-permute-start | bytes 393224 | tf_op jit(solution)/shard_map/ppermute | solution.py:246
  148.7 16.5 %collective-permute-start.21 = (bf16[256,512]{1,0:T(8,128)(2,1)S(1)}, bf16[256,512]{1,0:T(8,128)(2,1)S(1)}, u32[]{:S(2)}, u32[]{:S(2)}) collective-permute-start(bf16[256,512]{1,0:T(8,128)(2,1)S(1)} %pad_maximum_fusion.4), channel_id=1, source_target_pairs={{0,2},{1,3},{2,0},{3,1},{4,6},{5,7},{6,4},{7,5},{8,10},{9,11},{10,... | collective-permute-start | bytes 786440 | tf_op jit(solution)/shard_map/ppermute | solution.py:246
  153.0 8.4 %collective-permute-start.28 = (bf16[272,512]{1,0:T(8,128)(2,1)S(1)}, bf16[272,512]{1,0:T(8,128)(2,1)S(1)}, u32[]{:S(2)}, u32[]{:S(2)}) collective-permute-start(bf16[272,512]{1,0:T(8,128)(2,1)S(1)} %pad_maximum_fusion.3), channel_id=1, source_target_pairs={{0,4},{1,5},{2,6},{3,7},{4,0},{5,1},{6,2},{7,3},{8,12},{9,13},{10,... | collective-permute-start | bytes 835592 | tf_op jit(solution)/shard_map/ppermute | solution.py:246
  153.7 9.0 %collective-permute-start.26 = (bf16[272,512]{1,0:T(8,128)(2,1)S(1)}, bf16[272,512]{1,0:T(8,128)(2,1)S(1)}, u32[]{:S(2)}, u32[]{:S(2)}) collective-permute-start(bf16[272,512]{1,0:T(8,128)(2,1)S(1)} %pad_maximum_fusion.2), channel_id=1, source_target_pairs={{0,2},{1,3},{2,0},{3,1},{4,6},{5,7},{6,4},{7,5},{8,10},{9,11},{10,... | collective-permute-start | bytes 835592 | tf_op jit(solution)/shard_map/ppermute | solution.py:246
  155.4 9.8 %collective-permute-start.23 = (bf16[256,512]{1,0:T(8,128)(2,1)S(1)}, bf16[256,512]{1,0:T(8,128)(2,1)S(1)}, u32[]{:S(2)}, u32[]{:S(2)}) collective-permute-start(bf16[256,512]{1,0:T(8,128)(2,1)S(1)} %pad_maximum_fusion.5), channel_id=1, source_target_pairs={{0,4},{1,5},{2,6},{3,7},{4,0},{5,1},{6,2},{7,3},{8,12},{9,13},{10,... | collective-permute-start | bytes 786440 | tf_op jit(solution)/shard_map/ppermute | solution.py:246
  (13 other events, 115.3 us)
